TPU v7x, 32 devices: a whole 2x2x4 slice. The times are simulated.
32 devices in a mesh: surf: 8 (over y, x, core), norm: 4 (over z).
Axes of the slice: x: 2, y: 2, z: 4, core: 2. Of those that a mesh axis runs over, the one named last changes fastest.
Arguments:
- mode_shapes: bfloat16 [128, 64, 3, 256], P('surf'), may hold values from -6 to 6
- amplitude: float32 [128], replicated, may hold values from -0.046875 to 0.046875
- mode_patch: int32 [128], replicated, may hold values from 0 to 3
- column_patch: int32 [64, 256], replicated, may hold values from 0 to 3
- wall_mask: int32 [64, 256], P('surf'), may hold values 0 or 1
- offsets: int32 [64, 256], P('surf'), may hold values from 0 to 127
- coupling: float32 [64, 64, 256], P('norm', 'surf'), may hold values from 0.5 to 2
- pivot_inv: float32 [64, 64, 9, 256], P('norm', 'surf'), may hold values from -2 to 2
- stiffness: float32 [64, 64, 256], P('norm', 'surf'), may hold values from 0.00021972656 to 0.0005126953
Outputs:
- displacement: float32 [64, 64, 3, 256], P('norm', 'surf')
All inputs are finite; a program needn't handle non-finite values. No bound on the sum of `wall_mask` on one device may be relied on, other than what follows from the above.
Results may differ from a plain program's by a relative error of at most 0.0006.
Values may be sent and summed in bfloat16 or wider, within the bound.
A program may use at most 64 MiB of HBM per device.

v0:
```python
import functools

import jax
import jax.numpy as jnp
from jax import lax
from jax.experimental import pallas as pl
from jax.experimental.pallas import tpu as pltpu
from jax.sharding import PartitionSpec as P

SWEEPS = 3
MESH = pl.DeviceIdType.MESH


def loop(count, body, init, unroll=4):
    if count % unroll:
        unroll = 1

    def outer(step, carry):
        for part in range(unroll):
            carry = body(step * unroll + part, carry)
        return carry

    return lax.fori_loop(0, count // unroll, outer, init)


def later(count, body, init, unroll=5):
    return loop(count - 1, lambda step, carry: body(step + 1, carry), init, unroll)


def mat_vec(matrix, vector):
    return [
        matrix[3 * a] * vector[0] + matrix[3 * a + 1] * vector[1] + matrix[3 * a + 2] * vector[2]
        for a in range(3)
    ]


def mat_mat(left, right):
    return [
        left[3 * a] * right[b] + left[3 * a + 1] * right[3 + b] + left[3 * a + 2] * right[6 + b]
        for a in range(3)
        for b in range(3)
    ]


def added(left, right):
    return [a + b for a, b in zip(left, right)]


def planes(ref, index, count=3):
    return [ref[index, c] for c in range(count)]


def put(ref, index, values):
    for c, value in enumerate(values):
        ref[index, c] = value


def kernel(
    surf_size,
    norm_size,
    amplitude,
    mode_patch,
    column_patch,
    wall_mask,
    offsets,
    modes_hbm,
    coupling_hbm,
    pivot_hbm,
    stiffness_hbm,
    out,
    modes,
    coupling,
    pivot,
    stiffness,
    link,
    link_next,
    maps,
    end_map,
    part,
    got,
    mask_edge,
    wall,
    values,
    enter,
    edge_out,
    edge_in,
    halo,
    f_in,
    f_out,
    o_in,
    o_out,
    h_in,
    h_out,
    up_in,
    up_out,
    down_in,
    down_out,
    load_sem,
    part_send,
    part_recv,
    mask_send,
    mask_recv,
    link_send,
    link_recv,
    h_send,
    h_recv,
    up_send,
    up_recv,
    down_send,
    down_recv,
    f_send,
    f_recv,
    o_send,
    o_recv,
    edge_send,
    edge_recv,
):
    S, N = surf_size, norm_size
    K, _, R, W = pivot.shape
    M = modes.shape[0]
    B = 2 * R
    blocks = modes.shape[2] // B
    me = lax.axis_index("surf")
    place = lax.axis_index("norm")
    before = lax.rem(me + S - 1, S)
    after = lax.rem(me + 1, S)
    first, last = place == 0, place == N - 1

    def to_surf(src, dst, send, recv, target):
        return pltpu.make_async_remote_copy(
            src_ref=src, dst_ref=dst, send_sem=send, recv_sem=recv,
            device_id={"surf": target}, device_id_type=MESH,
        )

    def to_norm(src, dst, send, recv, target):
        return pltpu.make_async_remote_copy(
            src_ref=src, dst_ref=dst, send_sem=send, recv_sem=recv,
            device_id={"norm": target}, device_id_type=MESH,
        )

    mode_loads = [
        pltpu.make_async_copy(
            modes_hbm.at[:, :, pl.ds(b * B, B), :], modes.at[:, :, pl.ds(b * B, B), :], load_sem.at[3 + b]
        )
        for b in range(blocks)
    ]
    loads = [
        pltpu.make_async_copy(coupling_hbm, coupling, load_sem.at[0]),
        pltpu.make_async_copy(pivot_hbm, pivot, load_sem.at[1]),
        pltpu.make_async_copy(stiffness_hbm, stiffness, load_sem.at[2]),
    ]
    for copy in mode_loads + loads:
        copy.start()

    barrier = pltpu.get_barrier_semaphore()
    for hop in range(1, S):
        pl.semaphore_signal(
            barrier, inc=1, device_id={"surf": lax.rem(me + hop, S)}, device_id_type=MESH
        )

    for hop in range(1, N):
        pl.semaphore_signal(
            barrier, inc=1, device_id={"norm": lax.rem(place + hop, N)}, device_id_type=MESH
        )

    own_mode = me * M
    for b in range(blocks):
        mode_loads[b].wait()
        patch = column_patch[b * B : (b + 1) * B, :]

        def mode_step(m, sums):
            weight = jnp.where(
                patch == mode_patch[own_mode + m], amplitude[own_mode + m], jnp.float32(0)
            )
            return [
                sums[c] + weight * modes[m, c, b * B : (b + 1) * B, :].astype(jnp.float32)
                for c in range(3)
            ]

        sums = loop(M, mode_step, [jnp.zeros((B, W), jnp.float32)] * 3)
        for c in range(3):
            for side in range(2):
                dest = 2 * b + side
                block = sums[c][side * R : (side + 1) * R]
                part[dest, c] = block
                part[(dest + 1) % S, 3, c : c + 1, :] = block[R - 1 : R]
                part[(dest - 1) % S, 3, 3 + c : 4 + c, :] = block[0:1]

    pl.semaphore_wait(barrier, S + N - 2)

    def part_copy(hop):
        dest = lax.rem(me + hop, S)
        return to_surf(part.at[dest], got.at[hop], part_send.at[hop], part_recv.at[hop], dest)

    for hop in range(1, S):
        part_copy(hop).start()
    mask_up = to_surf(wall_mask, mask_edge.at[0], mask_send.at[0], mask_recv.at[0], after)
    mask_down = to_surf(wall_mask, mask_edge.at[1], mask_send.at[1], mask_recv.at[1], before)
    mask_up.start()
    mask_down.start()
    link_copy = to_norm(coupling_hbm.at[0], link_next, link_send, link_recv, place - 1)

    @pl.when(jnp.logical_not(first))
    def _():
        link_copy.start()

    for copy in loads:
        copy.wait()
    cut = offsets[...]
    base = place * K

    def link_step(k, carry):
        link[k] = jnp.where(cut == base + k, jnp.float32(0), coupling[k])
        return carry

    loop(K, link_step, 0)

    @pl.when(last)
    def _():
        link[K] = jnp.zeros((R, W), jnp.float32)

    def lower_step(k, state):
        scaled = [p * link[k] for p in planes(pivot, k, 9)]
        state = mat_mat(scaled, state)
        put(maps, k, state)
        return state

    first_map = [p * link[0] for p in planes(pivot, 0, 9)]
    put(maps, 0, first_map)
    ends = lax.fori_loop(1, K, lower_step, first_map)
    for c in range(9):
        end_map[c] = ends[c]

    @pl.when(jnp.logical_not(last))
    def _():
        link_copy.wait_recv()
        link[K] = jnp.where(cut == base + K, jnp.float32(0), link_next[...])

    def upper_step(step, state):
        k = K - 1 - step
        scaled = [p * link[k + 1] for p in planes(pivot, k, 9)]
        state = added(planes(maps, k, 9), mat_mat(scaled, state[:9])) + mat_mat(scaled, state[9:])
        put(maps, k, state)
        return state

    top_link = link[K]
    top_state = planes(maps, K - 1, 9) + [p * top_link for p in planes(pivot, K - 1, 9)]
    put(maps, K - 1, top_state)
    top_state = lax.fori_loop(1, K, upper_step, top_state)

    h_copy = to_norm(h_out, h_in, h_send, h_recv, place - 1)
    inside = jnp.logical_not(jnp.logical_or(first, last))

    def up_map(j):
        return to_norm(up_out.at[j], up_in.at[j], up_send.at[j], up_recv.at[j], place + 1)

    def down_map(j):
        return to_norm(down_out.at[j], down_in.at[j], down_send.at[j], down_recv.at[j], place - 1)

    def sends_up(j):
        return jnp.logical_and(place >= j, jnp.logical_not(last))

    def sends_down(j):
        return jnp.logical_and(N - 1 - place >= j, jnp.logical_not(first))

    @pl.when(last)
    def _():
        h_in[...] = jnp.zeros((9, R, W), jnp.float32)
        for c in range(9):
            h_out[c] = maps[0, c]
        h_copy.start()

    for j in range(1, min(2, N - 1)):

        @pl.when(sends_up(j))
        def _():
            put(up_out, j, [end_map[c] for c in range(9)])
            up_map(j).start()

        @pl.when(sends_down(j))
        def _():
            put(down_out, j, [maps[0, 9 + c] for c in range(9)])
            down_map(j).start()

    @pl.when(inside)
    def _():
        h_copy.wait_recv()
        inner = mat_mat([h_in[c] for c in range(9)], [end_map[c] for c in range(9)])
        whole = added(planes(maps, 0, 9), mat_mat([maps[0, 9 + c] for c in range(9)], inner))
        for c in range(9):
            h_out[c] = whole[c]
        h_copy.start()

    for j in range(2, N):

        @pl.when(place >= j)
        def _():
            up_map(j - 1).wait_recv()

        @pl.when(N - 1 - place >= j)
        def _():
            down_map(j - 1).wait_recv()

        if j < N - 1:

            @pl.when(sends_up(j))
            def _():
                put(up_out, j, mat_mat([end_map[c] for c in range(9)], planes(up_in, j - 1, 9)))
                up_map(j).start()

            @pl.when(sends_down(j))
            def _():
                put(
                    down_out, j,
                    mat_mat([maps[0, 9 + c] for c in range(9)], planes(down_in, j - 1, 9)),
                )
                down_map(j).start()

    total = [part[me, c] for c in range(4)]
    mask_up.wait_recv()
    mask_down.wait_recv()
    for hop in range(1, S):
        part_copy(hop).wait_recv()
        total = [total[c] + got[hop, c] for c in range(4)]
    mask = wall_mask[...].astype(jnp.float32)
    low_mask = mask_edge[0, R - 1 : R, :].astype(jnp.float32)
    high_mask = mask_edge[1, 0:1, :].astype(jnp.float32)
    row = lax.broadcasted_iota(jnp.int32, (R, W), 0)
    lane = lax.broadcasted_iota(jnp.int32, (R, W), 1)

    def around(x, low, high):
        nearby = jnp.where(row == 0, low, pltpu.roll(x, 1, 0))
        nearby += jnp.where(row == R - 1, high, pltpu.roll(x, R - 1, 0))
        nearby += jnp.where(lane == 0, jnp.float32(0), pltpu.roll(x, 1, 1))
        return nearby + jnp.where(lane == W - 1, jnp.float32(0), pltpu.roll(x, W - 1, 1))

    at_wall = jnp.where(first, jnp.float32(1), jnp.float32(0))
    for c in range(3):
        shift = total[c] * mask
        wall[c] = link[0] * shift * at_wall
        wall[3 + c] = around(
            shift, total[3][c : c + 1] * low_mask, total[3][3 + c : 4 + c] * high_mask
        )

    def edge_copies(sweep):
        return [
            to_surf(edge_out.at[sweep, 1], edge_in.at[sweep, 0], edge_send.at[sweep, 0], edge_recv.at[sweep, 0], after),
            to_surf(edge_out.at[sweep, 0], edge_in.at[sweep, 1], edge_send.at[sweep, 1], edge_recv.at[sweep, 1], before),
        ]

    def up_copy(sweep, j):
        return to_norm(
            f_out.at[sweep], f_in.at[sweep, j], f_send.at[sweep, j], f_recv.at[sweep, j], place + j
        )

    def down_copy(sweep, j):
        return to_norm(
            o_out.at[sweep], o_in.at[sweep, j], o_send.at[sweep, j], o_recv.at[sweep, j], place - j
        )

    for sweep in range(SWEEPS):
        if sweep > 0:
            for copy in edge_copies(sweep - 1):
                copy.wait_recv()
            for side in range(2):
                halo[side] = edge_in[sweep - 1, side].astype(jnp.float32)

        def source(k, sweep=sweep):
            if sweep == 0:
                blend = 1.0 - (base + k).astype(jnp.float32) / (K * N)
                factor = stiffness[k] * blend
                return [factor * wall[3 + c] for c in range(3)]
            return [
                stiffness[k]
                * around(out[k, c], halo[0, c, pl.ds(k, 1), :], halo[1, c, pl.ds(k, 1), :])
                for c in range(3)
            ]

        def forward(k, state):
            right = added(source(k), [link[k] * s for s in state])
            state = mat_vec(planes(pivot, k, 9), right)
            put(values, k, state)
            return state

        start = mat_vec(
            planes(pivot, 0, 9), added(source(0), [wall[c] for c in range(3)])
        )
        put(values, 0, start)
        ends = later(K, forward, start)

        def backward(step, state):
            k = K - 1 - step
            state = added(
                planes(values, k), mat_vec(planes(pivot, k, 9), [link[k + 1] * s for s in state])
            )
            put(values, k, state)
            return state

        tops = later(K, backward, ends)
        put(f_out, sweep, ends)
        for j in range(N - 1, 0, -1):

            @pl.when(place + j < N)
            def _():
                up_copy(sweep, j).start()

        if sweep == 0:

            @pl.when(first)
            def _():
                h_copy.wait_recv()

        @pl.when(jnp.logical_not(first))
        def _():
            top = added(
                tops,
                mat_vec(
                    [maps[0, 9 + c] for c in range(9)], mat_vec([h_in[c] for c in range(9)], ends)
                ),
            )
            put(o_out, sweep, top)
            for j in range(N - 1, 0, -1):

                @pl.when(place - j >= 0)
                def _():
                    down_copy(sweep, j).start()

        enter[...] = jnp.zeros(enter.shape, jnp.float32)
        for j in range(1, N):

            @pl.when(place - j >= 0)
            def _():
                up_copy(sweep, j).wait_recv()
                moved = planes(f_in.at[sweep], j)
                if j > 1:
                    moved = mat_vec(planes(up_in, j - 1, 9), moved)
                put(enter, 0, added(planes(enter, 0), moved))

            @pl.when(place + j < N)
            def _():
                down_copy(sweep, j).wait_recv()
                moved = planes(o_in.at[sweep], j)
                if j > 1:
                    moved = mat_vec(planes(down_in, j - 1, 9), moved)
                put(enter, 1, added(planes(enter, 1), moved))

        entering = planes(enter, 0)
        state = added(ends, mat_vec([end_map[c] for c in range(9)], entering))
        above = added(planes(enter, 1), mat_vec([h_in[c] for c in range(9)], state))

        def finish(k, carry, sweep=sweep):
            state = added(planes(values, k), mat_vec(planes(maps, k, 9), entering))
            state = added(state, mat_vec([maps[k, 9 + c] for c in range(9)], above))
            put(out, k, state)
            if sweep < SWEEPS - 1:
                for c in range(3):
                    halo[0, c, pl.ds(k, 1), :] = state[c][0:1]
                    halo[1, c, pl.ds(k, 1), :] = state[c][R - 1 : R]
            return carry

        loop(K, finish, 0, 4)
        if sweep < SWEEPS - 1:
            for side in range(2):
                edge_out[sweep, side] = halo[side].astype(jnp.bfloat16)
            for copy in edge_copies(sweep):
                copy.start()

    for hop in range(1, S):
        part_copy(hop).wait_send()
    mask_up.wait_send()
    mask_down.wait_send()
    for sweep in range(SWEEPS - 1):
        for copy in edge_copies(sweep):
            copy.wait_send()

    @pl.when(jnp.logical_not(first))
    def _():
        link_copy.wait_send()
        h_copy.wait_send()

    for j in range(1, N):
        if j < N - 1:

            @pl.when(sends_up(j))
            def _():
                up_map(j).wait_send()

            @pl.when(sends_down(j))
            def _():
                down_map(j).wait_send()

        for sweep in range(SWEEPS):

            @pl.when(place + j < N)
            def _():
                up_copy(sweep, j).wait_send()

            @pl.when(place - j >= 0)
            def _():
                down_copy(sweep, j).wait_send()


def per_device(
    surf_size, norm_size, mode_shapes, amplitude, mode_patch, column_patch, wall_mask, offsets,
    coupling, pivot_inv, stiffness,
):
    S, N = surf_size, norm_size
    modes = mode_shapes.transpose(0, 2, 1, 3)
    pivot = pivot_inv.transpose(0, 2, 1, 3)
    K, _, R, W = pivot.shape
    f32, bf16 = jnp.float32, jnp.bfloat16
    vmem = pl.BlockSpec(memory_space=pltpu.VMEM)
    smem = pl.BlockSpec(memory_space=pltpu.SMEM)
    hbm = pl.BlockSpec(memory_space=pl.ANY)
    dma = pltpu.SemaphoreType.DMA
    out = pl.pallas_call(
        functools.partial(kernel, surf_size, norm_size),
        out_shape=jax.ShapeDtypeStruct((K, 3, R, W), f32),
        in_specs=[smem, smem, vmem, vmem, vmem, hbm, hbm, hbm, hbm],
        out_specs=vmem,
        scratch_shapes=[
            pltpu.VMEM(modes.shape, bf16),
            pltpu.VMEM((K, R, W), f32),
            pltpu.VMEM((K, 9, R, W), f32),
            pltpu.VMEM((K, R, W), f32),
            pltpu.VMEM((K + 1, R, W), f32),
            pltpu.VMEM((R, W), f32),
            pltpu.VMEM((K, 18, R, W), f32),
            pltpu.VMEM((9, R, W), f32),
            pltpu.VMEM((S, 4, R, W), f32),
            pltpu.VMEM((S, 4, R, W), f32),
            pltpu.VMEM((2, R, W), jnp.int32),
            pltpu.VMEM((6, R, W), f32),
            pltpu.VMEM((K, 3, R, W), f32),
            pltpu.VMEM((2, 3, R, W), f32),
            pltpu.VMEM((SWEEPS - 1, 2, 3, K, W), bf16),
            pltpu.VMEM((SWEEPS - 1, 2, 3, K, W), bf16),
            pltpu.VMEM((2, 3, K, W), f32),
            pltpu.VMEM((SWEEPS, N, 3, R, W), f32),
            pltpu.VMEM((SWEEPS, 3, R, W), f32),
            pltpu.VMEM((SWEEPS, N, 3, R, W), f32),
            pltpu.VMEM((SWEEPS, 3, R, W), f32),
            pltpu.VMEM((9, R, W), f32),
            pltpu.VMEM((9, R, W), f32),
            pltpu.VMEM((N, 9, R, W), f32),
            pltpu.VMEM((N, 9, R, W), f32),
            pltpu.VMEM((N, 9, R, W), f32),
            pltpu.VMEM((N, 9, R, W), f32),
            dma((3 + modes.shape[2] // (2 * R),)),
            dma((S,)),
            dma((S,)),
            dma((2,)),
            dma((2,)),
            dma,
            dma,
            dma,
            dma,
            dma((N,)),
            dma((N,)),
            dma((N,)),
            dma((N,)),
            dma((SWEEPS, N)),
            dma((SWEEPS, N)),
            dma((SWEEPS, N)),
            dma((SWEEPS, N)),
            dma((SWEEPS - 1, 2)),
            dma((SWEEPS - 1, 2)),
        ],
        compiler_params=pltpu.CompilerParams(collective_id=0, has_side_effects=True),
        name="line_sweeps",
    )(amplitude, mode_patch, column_patch, wall_mask, offsets, modes, coupling, pivot, stiffness)
    return out.transpose(0, 2, 1, 3)


def solution(mesh):
    return jax.shard_map(
        functools.partial(per_device, mesh.shape["surf"], mesh.shape["norm"]),
        mesh=mesh,
        in_specs=(
            P("surf", None, None, None),
            P(),
            P(),
            P(),
            P("surf", None),
            P("surf", None),
            P("norm", "surf", None),
            P("norm", "surf", None, None),
            P("norm", "surf", None),
        ),
        out_specs=P("norm", "surf", None, None),
        check_vma=False,
    )
```

profile of v0, /device:TPU:0, one launch (start us, length us, event | category | flops | bytes accessed | tf_op | source)
XLA Modules:
  0.0 41.8 jit_solution(840929510857512643)
XLA Ops:
  0.0 40.0 %line_sweeps.1 = f32[16,3,8,256]{3,2,1,0:T(8,128)} custom-call(f32[128]{0:T(128)} %amplitude.1, s32[128]{0:T(128)} %mode_patch.1, s32[64,256]{1,0:T(8,128)} %column_patch.1, s32[8,256]{1,0:T(8,128)} %wall_mask.1, s32[8,256]{1,0:T(8,128)} %offsets.1, bf16[16,3,64,256]{3,2,1,0:T(8,128)(2,1)} %bitcast.3, f32[16,8,256]{2,1,0:T(8,128)} %coupling_hbm.1, ...), custom_call_target="tpu_custom_call" | custom-call | tf_op jit(solution)/shard_map/line_sweeps/pallas_call | solution.py:516
  40.0 1.8 %copy.11 = f32[16,8,3,256]{3,1,2,0:T(8,128)} copy(f32[16,8,3,256]{3,1,2,0:T(8,128)} %bitcast.4) | data formatting | bytes 786432
where the time goes:
time: 42 us; the launch traced here: 41.8 us
  Pallas kernels  40 us (95%)
  local copies, waits for them, and re-layouts  1.77 us (4%)
    pallas_call x1, Pallas kernels, per_device(): pl.pallas_call(functools.partial(kernel, surf_size, norm_size), out_shape...  40 us
    unnamed x1, local copies, waits for them, and re-layouts  1.77 us

commit v1 on v0

--- a/solution.py
+++ b/solution.py
@@ -515,7 +515,7 @@
     dma = pltpu.SemaphoreType.DMA
     out = pl.pallas_call(
         functools.partial(kernel, surf_size, norm_size),
-        out_shape=jax.ShapeDtypeStruct((K, 3, R, W), f32),
+        out_shape=pltpu.VMEM((K, 3, R, W), f32),
         in_specs=[smem, smem, vmem, vmem, vmem, hbm, hbm, hbm, hbm],
         out_specs=vmem,
         scratch_shapes=[

time: 42 us -> 40.2 us (0.957)
  local copies, waits for them, and re-layouts: 1.77 us -> 0.75 us
  Pallas kernels: 40 us -> 39.2 us
    unnamed x1, local copies, waits for them, and re-layouts: 1.77 us -> 0.75 us
    pallas_call x1, Pallas kernels: 40 us -> 39.2 us  [per_device(): pl.pallas_call(functools.partial(kernel, surf_size, norm_size), out_shape...]
where the time goes in v1:
time: 40.2 us; the launch traced here: 40 us
  Pallas kernels  39.2 us (98%)
  local copies, waits for them, and re-layouts  0.75 us (2%)
    pallas_call x1, Pallas kernels, per_device(): pl.pallas_call(functools.partial(kernel, surf_size, norm_size), out_shape...  39.2 us

profile of v1, /device:TPU:0, one launch (start us, length us, event | category | flops | bytes accessed | tf_op | source)
XLA Modules:
  0.0 40.0 jit_solution(5621131221650925640)
XLA Ops:
  0.0 39.2 %line_sweeps.1 = f32[16,3,8,256]{3,2,1,0:T(8,128)S(1)} custom-call(f32[128]{0:T(128)} %amplitude.1, s32[128]{0:T(128)} %mode_patch.1, s32[64,256]{1,0:T(8,128)} %column_patch.1, s32[8,256]{1,0:T(8,128)} %wall_mask.1, s32[8,256]{1,0:T(8,128)} %offsets.1, bf16[16,3,64,256]{3,2,1,0:T(8,128)(2,1)} %bitcast.4, f32[16,8,256]{2,1,0:T(8,128)} %coupling_hbm.1, ...), custom_call_target="tpu_custom_call" | custom-call | tf_op jit(solution)/shard_map/line_sweeps/pallas_call | solution.py:516
  39.2 0.7 %copy.11 = f32[16,8,3,256]{3,1,2,0:T(8,128)} copy(f32[16,8,3,256]{3,1,2,0:T(8,128)S(1)} %bitcast.3) | data formatting | bytes 786432

commit v2 on v1

v2 whole, which is shorter than its diff:
```python
import functools
import types

import jax
import jax.numpy as jnp
from jax import lax
from jax.experimental import pallas as pl
from jax.experimental.pallas import tpu as pltpu
from jax.sharding import PartitionSpec as P

SWEEPS = 3
LANES = 128
MESH = pl.DeviceIdType.MESH


def loop(count, body, init, unroll=4):
    if count % unroll:
        unroll = 1

    def outer(step, carry):
        for part in range(unroll):
            carry = body(step * unroll + part, carry)
        return carry

    return lax.fori_loop(0, count // unroll, outer, init)


def later(count, body, init, unroll=5):
    return loop(count - 1, lambda step, carry: body(step + 1, carry), init, unroll)


def mat_vec(matrix, vector):
    return [
        matrix[3 * a] * vector[0] + matrix[3 * a + 1] * vector[1] + matrix[3 * a + 2] * vector[2]
        for a in range(3)
    ]


def mat_mat(left, right):
    return [
        left[3 * a] * right[b] + left[3 * a + 1] * right[3 + b] + left[3 * a + 2] * right[6 + b]
        for a in range(3)
        for b in range(3)
    ]


def added(left, right):
    return [a + b for a, b in zip(left, right)]


def planes(ref, index, count=3):
    return [ref[index, c] for c in range(count)]


def whole(ref, count=9):
    return [ref[c] for c in range(count)]


def rows(ref, count=3):
    return [ref[c : c + 1, :] for c in range(count)]


def put(ref, index, values):
    for c, value in enumerate(values):
        ref[index, c] = value


def put_rows(ref, values):
    for c, value in enumerate(values):
        ref[c : c + 1, :] = value


def kernel(
    surf_size, norm_size, names,
    amplitude, mode_patch, column_patch, wall_mask, offsets,
    modes_hbm, coupling_hbm, pivot_hbm, stiffness_hbm,
    out, *scratch,
):
    s = types.SimpleNamespace(**dict(zip(names, scratch)))
    modes, coupling, pivot, stiffness = s.modes, s.coupling, s.pivot, s.stiffness
    link, maps, part, got, wall, values, halo = s.link, s.maps, s.part, s.got, s.wall, s.values, s.halo
    S, N = surf_size, norm_size
    K, _, R, W = pivot.shape
    M = modes.shape[0]
    B = 2 * R
    blocks = modes.shape[2] // B
    chunks = W // LANES
    me = lax.axis_index("surf")
    place = lax.axis_index("norm")
    before = lax.rem(me + S - 1, S)
    after = lax.rem(me + 1, S)
    first, last = place == 0, place == N - 1
    inside = jnp.logical_not(jnp.logical_or(first, last))
    base = place * K

    def to(src, dst, send, recv, **target):
        return pltpu.make_async_remote_copy(
            src_ref=src, dst_ref=dst, send_sem=send, recv_sem=recv,
            device_id=target, device_id_type=MESH,
        )

    def toward(side):
        return after if side == 0 else before

    mode_loads = [
        pltpu.make_async_copy(
            modes_hbm.at[:, :, pl.ds(b * B, B), :], modes.at[:, :, pl.ds(b * B, B), :], s.load_sem.at[3 + b]
        )
        for b in range(blocks)
    ]
    loads = [
        pltpu.make_async_copy(coupling_hbm, coupling, s.load_sem.at[0]),
        pltpu.make_async_copy(pivot_hbm, pivot, s.load_sem.at[1]),
        pltpu.make_async_copy(stiffness_hbm, stiffness, s.load_sem.at[2]),
    ]
    for copy in loads + mode_loads:
        copy.start()

    barrier = pltpu.get_barrier_semaphore()

    def greet(**target):
        pl.semaphore_signal(barrier, inc=1, device_id=target, device_id_type=MESH)

    for hop in range(1, S):
        greet(surf=lax.rem(me + hop, S))
    for hop in range(1, N):
        other = lax.rem(place + hop, N)
        greet(norm=other)
        greet(surf=before, norm=other)
        greet(surf=after, norm=other)

    for copy in loads:
        copy.wait()
    cut = offsets[...]

    def link_step(k, carry):
        link[k] = jnp.where(cut == base + k, jnp.float32(0), coupling[k])
        return carry

    loop(K, link_step, 0)

    def lower_step(k, state):
        scaled = [p * link[k] for p in planes(pivot, k, 9)]
        state = mat_mat(scaled, state)
        put(maps, k, state)
        return state

    first_map = [p * link[0] for p in planes(pivot, 0, 9)]
    put(maps, 0, first_map)
    ends = lax.fori_loop(1, K, lower_step, first_map)
    for c in range(9):
        s.end_map[c] = ends[c]

    def upper_step(step, state):
        k = K - 1 - step
        scaled = [p * link[k + 1] for p in planes(pivot, k, 9)]
        state = added(planes(maps, k, 9), mat_mat(scaled, state[:9])) + mat_mat(scaled, state[9:])
        put(maps, k, state)
        return state

    top_state = ends + planes(pivot, K - 1, 9)
    put(maps, K - 1, top_state)
    top_state = lax.fori_loop(1, K, upper_step, top_state)
    for c in range(18):
        s.top_map[c] = link[0] * top_state[c]

    own_mode = me * M
    for b in range(blocks):
        mode_loads[b].wait()
        patch = column_patch[b * B : (b + 1) * B, :]

        def mode_step(m, sums):
            weight = jnp.where(
                patch == mode_patch[own_mode + m], amplitude[own_mode + m], jnp.float32(0)
            )
            return [
                sums[c] + weight * modes[m, c, b * B : (b + 1) * B, :].astype(jnp.float32)
                for c in range(3)
            ]

        sums = loop(M, mode_step, [jnp.zeros((B, W), jnp.float32)] * 3)
        for c in range(3):
            for side in range(2):
                dest = 2 * b + side
                block = sums[c][side * R : (side + 1) * R]
                part[dest, c] = block
                part[(dest + 1) % S, 3, c : c + 1, :] = block[R - 1 : R]
                part[(dest - 1) % S, 3, 3 + c : 4 + c, :] = block[0:1]

    pl.semaphore_wait(barrier, S - 1 + 3 * (N - 1))

    def h_copy(q):
        return to(s.h_out.at[q], s.h_in.at[q], s.h_send.at[q], s.h_recv.at[q], norm=place - 1)

    def chunk(ref, q, start=0):
        return [ref[start + c, :, q * LANES : (q + 1) * LANES] for c in range(9)]

    def h_full():
        return [jnp.concatenate([s.h_in[q, c] for q in range(chunks)], axis=1) for c in range(9)]

    def row_copy(slot, side, step):
        return to(
            s.row_out.at[slot, side], s.row_in.at[slot, side],
            s.row_send.at[slot, side], s.row_recv.at[slot, side],
            surf=toward(side), norm=place + step,
        )

    def send_rows(slot, step, values9):
        put_rows(s.row_out.at[slot, 0], [v[R - 1 : R] for v in values9])
        put_rows(s.row_out.at[slot, 1], [v[0:1] for v in values9])
        for side in range(2):
            row_copy(slot, side, step).start()

    UP, DOWN, ENDS, TOP = 0, N, 0, N

    def up_map(j):
        return to(s.up_out.at[j], s.up_in.at[j], s.up_send.at[j], s.up_recv.at[j], norm=place + 1)

    def down_map(j):
        return to(s.down_out.at[j], s.down_in.at[j], s.down_send.at[j], s.down_recv.at[j], norm=place - 1)

    def sends_up(j):
        return jnp.logical_and(place >= j, jnp.logical_not(last))

    def sends_down(j):
        return jnp.logical_and(N - 1 - place >= j, jnp.logical_not(first))

    @pl.when(last)
    def _():
        s.h_in[...] = jnp.zeros(s.h_in.shape, jnp.float32)
        s.row_in[TOP] = jnp.zeros(s.row_in.shape[1:], jnp.float32)
        for q in range(chunks):
            put(s.h_out, q, chunk(s.top_map, q))
            h_copy(q).start()

    def part_copy(hop):
        dest = lax.rem(me + hop, S)
        return to(part.at[dest], got.at[hop], s.part_send.at[hop], s.part_recv.at[hop], surf=dest)

    for hop in range(1, S):
        part_copy(hop).start()
    mask_up = to(wall_mask, s.mask_edge.at[0], s.mask_send.at[0], s.mask_recv.at[0], surf=after)
    mask_down = to(wall_mask, s.mask_edge.at[1], s.mask_send.at[1], s.mask_recv.at[1], surf=before)
    mask_up.start()
    mask_down.start()

    for j in range(1, min(2, N - 1)):

        @pl.when(sends_up(j))
        def _():
            value = whole(s.end_map)
            put(s.up_out, j, value)
            up_map(j).start()
            send_rows(UP + j, 1, value)

        @pl.when(sends_down(j))
        def _():
            value = [s.top_map[9 + c] for c in range(9)]
            put(s.down_out, j, value)
            down_map(j).start()
            send_rows(DOWN + j, -1, value)

    @pl.when(last)
    def _():
        send_rows(TOP, -1, whole(s.top_map))

    send_rows(ENDS, 0, whole(s.end_map))

    def pack_step(k, carry):
        for c in range(18):
            value = maps[k, c]
            s.side_rows[0, c, pl.ds(k, 1), :] = value[R - 1 : R]
            s.side_rows[1, c, pl.ds(k, 1), :] = value[0:1]
        return carry

    loop(K, pack_step, 0, 2)

    def side_map_copy(side):
        return to(
            s.side_out.at[side], s.side_in.at[side], s.side_send.at[side], s.side_recv.at[side],
            surf=toward(side),
        )

    for side in range(2):
        for c in range(18):
            s.side_out[side, c] = s.side_rows[side, c].astype(jnp.bfloat16)
        side_map_copy(side).start()

    def relay():
        for q in range(chunks):
            h_copy(q).wait_recv()
            inner = mat_mat(whole(s.h_in.at[q]), chunk(s.end_map, q))
            value = added(chunk(s.top_map, q), mat_mat(chunk(s.top_map, q, 9), inner))
            put(s.h_out, q, value)
            h_copy(q).start()
            for c in range(9):
                s.row_out[TOP, 0, c : c + 1, q * LANES : (q + 1) * LANES] = value[c][R - 1 : R]
                s.row_out[TOP, 1, c : c + 1, q * LANES : (q + 1) * LANES] = value[c][0:1]
        for side in range(2):
            row_copy(TOP, side, -1).start()

    early = jnp.logical_and(inside, place == N - 2)

    @pl.when(early)
    def _():
        relay()

    for j in range(2, N - 1):

        @pl.when(sends_up(j))
        def _():
            up_map(j - 1).wait_recv()
            value = mat_mat(whole(s.end_map), planes(s.up_in, j - 1, 9))
            put(s.up_out, j, value)
            up_map(j).start()
            send_rows(UP + j, 1, value)

        @pl.when(sends_down(j))
        def _():
            down_map(j - 1).wait_recv()
            value = mat_mat([s.top_map[9 + c] for c in range(9)], planes(s.down_in, j - 1, 9))
            put(s.down_out, j, value)
            down_map(j).start()
            send_rows(DOWN + j, -1, value)

    total = [part[me, c] for c in range(4)]
    mask_up.wait_recv()
    mask_down.wait_recv()
    for hop in range(1, S):
        part_copy(hop).wait_recv()
        total = [total[c] + got[hop, c] for c in range(4)]
    mask = wall_mask[...].astype(jnp.float32)
    low_mask = s.mask_edge[0, R - 1 : R, :].astype(jnp.float32)
    high_mask = s.mask_edge[1, 0:1, :].astype(jnp.float32)
    row = lax.broadcasted_iota(jnp.int32, (R, W), 0)
    lane = lax.broadcasted_iota(jnp.int32, (R, W), 1)

    def around(x, low, high):
        nearby = jnp.where(row == 0, low, pltpu.roll(x, 1, 0))
        nearby += jnp.where(row == R - 1, high, pltpu.roll(x, R - 1, 0))
        nearby += jnp.where(lane == 0, jnp.float32(0), pltpu.roll(x, 1, 1))
        return nearby + jnp.where(lane == W - 1, jnp.float32(0), pltpu.roll(x, W - 1, 1))

    at_wall = jnp.where(first, jnp.float32(1), jnp.float32(0))
    for c in range(3):
        shift = total[c] * mask
        wall[c] = link[0] * shift * at_wall
        wall[3 + c] = around(
            shift, total[3][c : c + 1] * low_mask, total[3][3 + c : 4 + c] * high_mask
        )

    def edge_copy(sweep, side):
        return to(
            s.edge_out.at[sweep, side], s.edge_in.at[sweep, side],
            s.edge_send.at[sweep, side], s.edge_recv.at[sweep, side], surf=toward(side),
        )

    def up_copy(sweep, j):
        return to(
            s.f_out.at[sweep], s.f_in.at[sweep, j], s.f_send.at[sweep, j], s.f_recv.at[sweep, j],
            norm=place + j,
        )

    def down_copy(sweep, j):
        return to(
            s.o_out.at[sweep], s.o_in.at[sweep, j], s.o_send.at[sweep, j], s.o_recv.at[sweep, j],
            norm=place - j,
        )

    def up_edge(sweep, side, j):
        return to(
            s.fe_out.at[sweep, side], s.fe_in.at[sweep, side, j],
            s.fe_send.at[sweep, side, j], s.fe_recv.at[sweep, side, j],
            surf=toward(side), norm=place + j,
        )

    def down_edge(sweep, side, j):
        return to(
            s.oe_out.at[sweep, side], s.oe_in.at[sweep, side, j],
            s.oe_send.at[sweep, side, j], s.oe_recv.at[sweep, side, j],
            surf=toward(side), norm=place - j,
        )

    for sweep in range(SWEEPS):
        shared = sweep < SWEEPS - 1

        def source(k, sweep=sweep):
            if sweep == 0:
                blend = 1.0 - (base + k).astype(jnp.float32) / (K * N)
                factor = stiffness[k] * blend
                return [factor * wall[3 + c] for c in range(3)]
            return [
                stiffness[k]
                * around(out[k, c], halo[0, c, pl.ds(k, 1), :], halo[1, c, pl.ds(k, 1), :])
                for c in range(3)
            ]

        def forward(k, state):
            right = added(source(k), [link[k] * v for v in state])
            state = mat_vec(planes(pivot, k, 9), right)
            put(values, k, state)
            return state

        start = mat_vec(
            planes(pivot, 0, 9), added(source(0), [wall[c] for c in range(3)])
        )
        put(values, 0, start)
        ends = later(K, forward, start)
        put(s.f_out, sweep, ends)
        for j in range(N - 1, 0, -1):

            @pl.when(place + j < N)
            def _():
                up_copy(sweep, j).start()

        if shared:
            put_rows(s.fe_out.at[sweep, 0], [v[R - 1 : R] for v in ends])
            put_rows(s.fe_out.at[sweep, 1], [v[0:1] for v in ends])
            for j in range(N - 1, -1, -1):

                @pl.when(place + j < N)
                def _():
                    for side in range(2):
                        up_edge(sweep, side, j).start()

        def keep(k, state):
            put(values, k, state)
            if shared:
                for c in range(3):
                    halo[0, c, pl.ds(k, 1), :] = state[c][R - 1 : R]
                    halo[1, c, pl.ds(k, 1), :] = state[c][0:1]

        def backward(step, state):
            k = K - 1 - step
            state = added(
                planes(values, k), mat_vec(planes(pivot, k, 9), [link[k + 1] * v for v in state])
            )
            keep(k, state)
            return state

        keep(K - 1, ends)
        tops = later(K, backward, ends)

        if sweep == 0:

            @pl.when(jnp.logical_and(inside, jnp.logical_not(early)))
            def _():
                relay()

        @pl.when(jnp.logical_not(first))
        def _():
            top = added(
                [link[0] * v for v in tops],
                mat_vec([s.top_map[9 + c] for c in range(9)], mat_vec(h_full(), ends)),
            )
            put(s.o_out, sweep, top)
            for j in range(N - 1, 0, -1):

                @pl.when(place - j >= 0)
                def _():
                    down_copy(sweep, j).start()

            if shared:
                put_rows(s.oe_out.at[sweep, 0], [v[R - 1 : R] for v in top])
                put_rows(s.oe_out.at[sweep, 1], [v[0:1] for v in top])
                for j in range(N - 1, 0, -1):

                    @pl.when(place - j >= 0)
                    def _():
                        for side in range(2):
                            down_edge(sweep, side, j).start()

        if shared:
            for side in range(2):
                s.edge_out[sweep, side] = halo[side].astype(jnp.bfloat16)
                edge_copy(sweep, side).start()

        s.enter[...] = jnp.zeros(s.enter.shape, jnp.float32)
        for j in range(1, N):
            if sweep == 0 and j > 1:

                @pl.when(jnp.logical_and(last, place >= j))
                def _():
                    up_map(j - 1).wait_recv()

                @pl.when(jnp.logical_and(first, N - 1 - place >= j))
                def _():
                    down_map(j - 1).wait_recv()

            @pl.when(place - j >= 0)
            def _():
                up_copy(sweep, j).wait_recv()
                moved = planes(s.f_in.at[sweep], j)
                if j > 1:
                    moved = mat_vec(planes(s.up_in, j - 1, 9), moved)
                put(s.enter, 0, added(planes(s.enter, 0), moved))

            @pl.when(place + j < N)
            def _():
                down_copy(sweep, j).wait_recv()
                moved = planes(s.o_in.at[sweep], j)
                if j > 1:
                    moved = mat_vec(planes(s.down_in, j - 1, 9), moved)
                put(s.enter, 1, added(planes(s.enter, 1), moved))

        if sweep == 0:

            @pl.when(first)
            def _():
                for q in range(chunks):
                    h_copy(q).wait_recv()

        entering = planes(s.enter, 0)
        state = added(ends, mat_vec(whole(s.end_map), entering))
        above = added(planes(s.enter, 1), mat_vec(h_full(), state))

        def finish(k, carry):
            state = added(planes(values, k), mat_vec(planes(maps, k, 9), entering))
            state = added(state, mat_vec([maps[k, 9 + c] for c in range(9)], above))
            put(out, k, state)
            return carry

        loop(K, finish, 0, 4)

        if shared:
            if sweep == 0:
                for side in range(2):
                    side_map_copy(side).wait_recv()
                    row_copy(ENDS, side, 0).wait_recv()

                @pl.when(jnp.logical_not(last))
                def _():
                    for side in range(2):
                        row_copy(TOP, side, 0).wait_recv()

                for j in range(2, N):

                    @pl.when(place >= j)
                    def _():
                        for side in range(2):
                            row_copy(UP + j - 1, side, 0).wait_recv()

                    @pl.when(N - 1 - place >= j)
                    def _():
                        for side in range(2):
                            row_copy(DOWN + j - 1, side, 0).wait_recv()

            s.enter_row[...] = jnp.zeros(s.enter_row.shape, jnp.float32)
            for j in range(1, N):

                @pl.when(place - j >= 0)
                def _():
                    for side in range(2):
                        up_edge(sweep, side, j).wait_recv()
                        moved = rows(s.fe_in.at[sweep, side, j])
                        if j > 1:
                            moved = mat_vec(rows(s.row_in.at[UP + j - 1, side], 9), moved)
                        put_rows(s.enter_row.at[side, 0], added(rows(s.enter_row.at[side, 0]), moved))

                @pl.when(place + j < N)
                def _():
                    for side in range(2):
                        down_edge(sweep, side, j).wait_recv()
                        moved = rows(s.oe_in.at[sweep, side, j])
                        if j > 1:
                            moved = mat_vec(rows(s.row_in.at[DOWN + j - 1, side], 9), moved)
                        put_rows(s.enter_row.at[side, 1], added(rows(s.enter_row.at[side, 1]), moved))

            for side in range(2):
                up_edge(sweep, side, 0).wait_recv()
                edge_copy(sweep, side).wait_recv()
                entered = rows(s.enter_row.at[side, 0])
                state = added(
                    rows(s.fe_in.at[sweep, side, 0]),
                    mat_vec(rows(s.row_in.at[ENDS, side], 9), entered),
                )
                higher = added(
                    rows(s.enter_row.at[side, 1]), mat_vec(rows(s.row_in.at[TOP, side], 9), state)
                )
                for c in range(3):
                    value = s.edge_in[sweep, side, c].astype(jnp.float32)
                    for b in range(3):
                        value += s.side_in[side, 3 * c + b].astype(jnp.float32) * entered[b]
                        value += s.side_in[side, 9 + 3 * c + b].astype(jnp.float32) * higher[b]
                    halo[side, c] = value

    for hop in range(1, S):
        part_copy(hop).wait_send()
    mask_up.wait_send()
    mask_down.wait_send()
    for side in range(2):
        side_map_copy(side).wait_send()
        row_copy(ENDS, side, 0).wait_send()
        for sweep in range(SWEEPS - 1):
            edge_copy(sweep, side).wait_send()

    @pl.when(jnp.logical_not(first))
    def _():
        for q in range(chunks):
            h_copy(q).wait_send()
        for side in range(2):
            row_copy(TOP, side, 0).wait_send()

    for j in range(1, N - 1):

        @pl.when(sends_up(j))
        def _():
            up_map(j).wait_send()
            for side in range(2):
                row_copy(UP + j, side, 0).wait_send()

        @pl.when(sends_down(j))
        def _():
            down_map(j).wait_send()
            for side in range(2):
                row_copy(DOWN + j, side, 0).wait_send()

    for j in range(N):

        @pl.when(place + j < N)
        def _():
            for sweep in range(SWEEPS):
                if j > 0:
                    up_copy(sweep, j).wait_send()
                if sweep < SWEEPS - 1:
                    for side in range(2):
                        up_edge(sweep, side, j).wait_send()

        if j > 0:

            @pl.when(place - j >= 0)
            def _():
                for sweep in range(SWEEPS):
                    down_copy(sweep, j).wait_send()
                    if sweep < SWEEPS - 1:
                        for side in range(2):
                            down_edge(sweep, side, j).wait_send()


def per_device(
    surf_size, norm_size, mode_shapes, amplitude, mode_patch, column_patch, wall_mask, offsets,
    coupling, pivot_inv, stiffness,
):
    S, N = surf_size, norm_size
    modes = mode_shapes.transpose(0, 2, 1, 3)
    pivot = pivot_inv.transpose(0, 2, 1, 3)
    K, _, R, W = pivot.shape
    C = W // LANES
    f32, bf16 = jnp.float32, jnp.bfloat16
    vmem = pl.BlockSpec(memory_space=pltpu.VMEM)
    smem = pl.BlockSpec(memory_space=pltpu.SMEM)
    hbm = pl.BlockSpec(memory_space=pltpu.HBM)
    dma = pltpu.SemaphoreType.DMA

    def room(*shape):
        return pltpu.VMEM(shape, f32)

    def half(*shape):
        return pltpu.VMEM(shape, bf16)

    G = SWEEPS - 1
    scratch = dict(
        modes=half(*modes.shape),
        coupling=room(K, R, W),
        pivot=room(K, 9, R, W),
        stiffness=room(K, R, W),
        link=room(K, R, W),
        maps=room(K, 18, R, W),
        end_map=room(9, R, W),
        top_map=room(18, R, W),
        part=room(S, 4, R, W),
        got=room(S, 4, R, W),
        mask_edge=pltpu.VMEM((2, R, W), jnp.int32),
        wall=room(6, R, W),
        values=room(K, 3, R, W),
        enter=room(2, 3, R, W),
        enter_row=room(2, 2, 3, W),
        halo=room(2, 3, K, W),
        edge_out=half(G, 2, 3, K, W),
        edge_in=half(G, 2, 3, K, W),
        side_rows=room(2, 18, K, W),
        side_out=half(2, 18, K, W),
        side_in=half(2, 18, K, W),
        row_out=room(2 * N, 2, 9, W),
        row_in=room(2 * N, 2, 9, W),
        f_in=room(SWEEPS, N, 3, R, W),
        f_out=room(SWEEPS, 3, R, W),
        o_in=room(SWEEPS, N, 3, R, W),
        o_out=room(SWEEPS, 3, R, W),
        fe_in=room(G, 2, N, 3, W),
        fe_out=room(G, 2, 3, W),
        oe_in=room(G, 2, N, 3, W),
        oe_out=room(G, 2, 3, W),
        h_in=room(C, 9, R, LANES),
        h_out=room(C, 9, R, LANES),
        up_in=room(N, 9, R, W),
        up_out=room(N, 9, R, W),
        down_in=room(N, 9, R, W),
        down_out=room(N, 9, R, W),
        load_sem=dma((3 + modes.shape[2] // (2 * R),)),
    )
    sems = dict(
        part=(S,), mask=(2,), h=(C,), row=(2 * N, 2), side=(2,), up=(N,), down=(N,),
        f=(SWEEPS, N), o=(SWEEPS, N), fe=(G, 2, N), oe=(G, 2, N), edge=(G, 2),
    )
    for name, shape in sems.items():
        scratch[name + "_send"] = dma(shape)
        scratch[name + "_recv"] = dma(shape)
    out = pl.pallas_call(
        functools.partial(kernel, S, N, tuple(scratch)),
        out_shape=pltpu.VMEM((K, 3, R, W), f32),
        in_specs=[smem, smem, vmem, vmem, vmem, hbm, hbm, hbm, hbm],
        out_specs=vmem,
        scratch_shapes=list(scratch.values()),
        compiler_params=pltpu.CompilerParams(
            collective_id=0, has_side_effects=True, vmem_limit_bytes=62 * 1024 * 1024
        ),
        name="line_sweeps",
    )(amplitude, mode_patch, column_patch, wall_mask, offsets, modes, coupling, pivot, stiffness)
    return out.transpose(0, 2, 1, 3)


def solution(mesh):
    return jax.shard_map(
        functools.partial(per_device, mesh.shape["surf"], mesh.shape["norm"]),
        mesh=mesh,
        in_specs=(
            P("surf", None, None, None),
            P(),
            P(),
            P(),
            P("surf", None),
            P("surf", None),
            P("norm", "surf", None),
            P("norm", "surf", None, None),
            P("norm", "surf", None),
        ),
        out_specs=P("norm", "surf", None, None),
        check_vma=False,
    )
```

time: 40.2 us -> 32.9 us (0.82)
  Pallas kernels: 39.2 us -> 32 us
    pallas_call x1, Pallas kernels: 39.2 us -> 32 us  [per_device(): pl.pallas_call(functools.partial(kernel, S, N, tuple(scratch)), out_shape...]
where the time goes in v2:
time: 32.9 us; the launch traced here: 32.8 us
  Pallas kernels  32 us (97%)
  local copies, waits for them, and re-layouts  0.75 us (2%)
    pallas_call x1, Pallas kernels, per_device(): pl.pallas_call(functools.partial(kernel, S, N, tuple(scratch)), out_shape...  32 us
    unnamed x1, local copies, waits for them, and re-layouts  0.75 us

profile of v2, /device:TPU:0, one launch (start us, length us, event | category | flops | bytes accessed | tf_op | source)
XLA Modules:
  0.0 32.8 jit_solution(14194856711705557689)
XLA Ops:
  0.0 32.0 %line_sweeps.1 = f32[16,3,8,256]{3,2,1,0:T(8,128)S(1)} custom-call(f32[128]{0:T(128)} %amplitude.1, s32[128]{0:T(128)} %mode_patch.1, s32[64,256]{1,0:T(8,128)} %column_patch.1, s32[8,256]{1,0:T(8,128)} %wall_mask.1, s32[8,256]{1,0:T(8,128)} %offsets.1, bf16[16,3,64,256]{3,2,1,0:T(8,128)(2,1)} %bitcast.4, f32[16,8,256]{2,1,0:T(8,128)} %coupling_hbm.1, ...), custom_call_target="tpu_custom_call" | custom-call | tf_op jit(solution)/shard_map/line_sweeps/pallas_call | solution.py:709
  32.0 0.7 %copy.11 = f32[16,8,3,256]{3,1,2,0:T(8,128)} copy(f32[16,8,3,256]{3,1,2,0:T(8,128)S(1)} %bitcast.3) | data formatting | bytes 786432

commit v3 on v2

--- a/solution.py
+++ b/solution.py
@@ -381,6 +381,16 @@
             surf=toward(side), norm=place - j,
         )
 
+    def change(send, sent, sweep, values3):
+        for c in range(3):
+            known = sent[c] if sweep > 0 else jnp.float32(0)
+            step = (values3[c] - known).astype(jnp.bfloat16)
+            send[sweep, c] = step
+            sent[c] = known + step.astype(jnp.float32)
+
+    def wide(ref, index):
+        return [v.astype(jnp.float32) for v in planes(ref, index)]
+
     for sweep in range(SWEEPS):
         shared = sweep < SWEEPS - 1
 
@@ -406,22 +416,22 @@
         )
         put(values, 0, start)
         ends = later(K, forward, start)
-        put(s.f_out, sweep, ends)
-        for j in range(N - 1, 0, -1):
-
-            @pl.when(place + j < N)
-            def _():
-                up_copy(sweep, j).start()
-
         if shared:
             put_rows(s.fe_out.at[sweep, 0], [v[R - 1 : R] for v in ends])
             put_rows(s.fe_out.at[sweep, 1], [v[0:1] for v in ends])
-            for j in range(N - 1, -1, -1):
+            for j in range(N - 1, 0, -1):
 
                 @pl.when(place + j < N)
                 def _():
                     for side in range(2):
                         up_edge(sweep, side, j).start()
+
+        change(s.f_out, s.f_sent, sweep, ends)
+        for j in range(N - 1, 0, -1):
+
+            @pl.when(place + j < N)
+            def _():
+                up_copy(sweep, j).start()
 
         def keep(k, state):
             put(values, k, state)
@@ -453,13 +463,6 @@
                 [link[0] * v for v in tops],
                 mat_vec([s.top_map[9 + c] for c in range(9)], mat_vec(h_full(), ends)),
             )
-            put(s.o_out, sweep, top)
-            for j in range(N - 1, 0, -1):
-
-                @pl.when(place - j >= 0)
-                def _():
-                    down_copy(sweep, j).start()
-
             if shared:
                 put_rows(s.oe_out.at[sweep, 0], [v[R - 1 : R] for v in top])
                 put_rows(s.oe_out.at[sweep, 1], [v[0:1] for v in top])
@@ -470,12 +473,22 @@
                         for side in range(2):
                             down_edge(sweep, side, j).start()
 
+            change(s.o_out, s.o_sent, sweep, top)
+            for j in range(N - 1, 0, -1):
+
+                @pl.when(place - j >= 0)
+                def _():
+                    down_copy(sweep, j).start()
+
         if shared:
             for side in range(2):
                 s.edge_out[sweep, side] = halo[side].astype(jnp.bfloat16)
                 edge_copy(sweep, side).start()
-
-        s.enter[...] = jnp.zeros(s.enter.shape, jnp.float32)
+                up_edge(sweep, side, 0).start()
+
+        if sweep == 0:
+            s.enter[...] = jnp.zeros(s.enter.shape, jnp.float32)
+
         for j in range(1, N):
             if sweep == 0 and j > 1:
 
@@ -490,7 +503,7 @@
             @pl.when(place - j >= 0)
             def _():
                 up_copy(sweep, j).wait_recv()
-                moved = planes(s.f_in.at[sweep], j)
+                moved = wide(s.f_in.at[sweep], j)
                 if j > 1:
                     moved = mat_vec(planes(s.up_in, j - 1, 9), moved)
                 put(s.enter, 0, added(planes(s.enter, 0), moved))
@@ -498,7 +511,7 @@
             @pl.when(place + j < N)
             def _():
                 down_copy(sweep, j).wait_recv()
-                moved = planes(s.o_in.at[sweep], j)
+                moved = wide(s.o_in.at[sweep], j)
                 if j > 1:
                     moved = mat_vec(planes(s.down_in, j - 1, 9), moved)
                 put(s.enter, 1, added(planes(s.enter, 1), moved))
@@ -683,10 +696,12 @@
         side_in=half(2, 18, K, W),
         row_out=room(2 * N, 2, 9, W),
         row_in=room(2 * N, 2, 9, W),
-        f_in=room(SWEEPS, N, 3, R, W),
-        f_out=room(SWEEPS, 3, R, W),
-        o_in=room(SWEEPS, N, 3, R, W),
-        o_out=room(SWEEPS, 3, R, W),
+        f_in=half(SWEEPS, N, 3, R, W),
+        f_out=half(SWEEPS, 3, R, W),
+        f_sent=room(3, R, W),
+        o_in=half(SWEEPS, N, 3, R, W),
+        o_out=half(SWEEPS, 3, R, W),
+        o_sent=room(3, R, W),
         fe_in=room(G, 2, N, 3, W),
         fe_out=room(G, 2, 3, W),
         oe_in=room(G, 2, N, 3, W),

time: 32.9 us -> 31.3 us (0.951)
  Pallas kernels: 32 us -> 30.4 us
    pallas_call x1, Pallas kernels: 32 us -> 30.4 us  [per_device(): pl.pallas_call(functools.partial(kernel, S, N, tuple(scratch)), out_shape...]
where the time goes in v3:
time: 31.3 us; the launch traced here: 31.1 us
  Pallas kernels  30.4 us (97%)
  local copies, waits for them, and re-layouts  0.75 us (2%)
    pallas_call x1, Pallas kernels, per_device(): pl.pallas_call(functools.partial(kernel, S, N, tuple(scratch)), out_shape...  30.4 us
    unnamed x1, local copies, waits for them, and re-layouts  0.75 us

profile of v3, /device:TPU:0, one launch (start us, length us, event | category | flops | bytes accessed | tf_op | source)
XLA Modules:
  0.0 31.1 jit_solution(12317501394415676926)
XLA Ops:
  0.0 30.4 %line_sweeps.1 = f32[16,3,8,256]{3,2,1,0:T(8,128)S(1)} custom-call(f32[128]{0:T(128)} %amplitude.1, s32[128]{0:T(128)} %mode_patch.1, s32[64,256]{1,0:T(8,128)} %column_patch.1, s32[8,256]{1,0:T(8,128)} %wall_mask.1, s32[8,256]{1,0:T(8,128)} %offsets.1, bf16[16,3,64,256]{3,2,1,0:T(8,128)(2,1)} %bitcast.4, f32[16,8,256]{2,1,0:T(8,128)} %coupling_hbm.1, ...), custom_call_target="tpu_custom_call" | custom-call | tf_op jit(solution)/shard_map/line_sweeps/pallas_call | solution.py:724
  30.4 0.7 %copy.11 = f32[16,8,3,256]{3,1,2,0:T(8,128)} copy(f32[16,8,3,256]{3,1,2,0:T(8,128)S(1)} %bitcast.3) | data formatting | bytes 786432

commit v4 on v3

--- a/solution.py
+++ b/solution.py
@@ -32,6 +32,14 @@
 def mat_vec(matrix, vector):
     return [
         matrix[3 * a] * vector[0] + matrix[3 * a + 1] * vector[1] + matrix[3 * a + 2] * vector[2]
+        for a in range(3)
+    ]
+
+
+def fold(start, matrix, vector):
+    return [
+        (start[a] + matrix[3 * a] * vector[0])
+        + (matrix[3 * a + 1] * vector[1] + matrix[3 * a + 2] * vector[2])
         for a in range(3)
     ]
 
@@ -141,6 +149,7 @@
 
     def lower_step(k, state):
         scaled = [p * link[k] for p in planes(pivot, k, 9)]
+        put(s.rise, k, scaled)
         state = mat_mat(scaled, state)
         put(maps, k, state)
         return state
@@ -154,6 +163,7 @@
     def upper_step(step, state):
         k = K - 1 - step
         scaled = [p * link[k + 1] for p in planes(pivot, k, 9)]
+        put(s.fall, k, scaled)
         state = added(planes(maps, k, 9), mat_mat(scaled, state[:9])) + mat_mat(scaled, state[9:])
         put(maps, k, state)
         return state
@@ -192,11 +202,19 @@
     def h_copy(q):
         return to(s.h_out.at[q], s.h_in.at[q], s.h_send.at[q], s.h_recv.at[q], norm=place - 1)
 
+    full_copy = to(s.full_out, s.full_in, s.full_send, s.full_recv, norm=place - 1)
+
     def chunk(ref, q, start=0):
         return [ref[start + c, :, q * LANES : (q + 1) * LANES] for c in range(9)]
 
-    def h_full():
-        return [jnp.concatenate([s.h_in[q, c] for q in range(chunks)], axis=1) for c in range(9)]
+    def h_part(q):
+        return [s.h_in[q, c].astype(jnp.float32) for c in range(9)]
+
+    def h_full(sweep):
+        if sweep > 0:
+            return whole(s.full_in)
+        pieces = [h_part(q) for q in range(chunks)]
+        return [jnp.concatenate([p[c] for p in pieces], axis=1) for c in range(9)]
 
     def row_copy(slot, side, step):
         return to(
@@ -227,10 +245,11 @@
 
     @pl.when(last)
     def _():
-        s.h_in[...] = jnp.zeros(s.h_in.shape, jnp.float32)
+        s.h_in[...] = jnp.zeros(s.h_in.shape, jnp.bfloat16)
+        s.full_in[...] = jnp.zeros(s.full_in.shape, jnp.float32)
         s.row_in[TOP] = jnp.zeros(s.row_in.shape[1:], jnp.float32)
         for q in range(chunks):
-            put(s.h_out, q, chunk(s.top_map, q))
+            put(s.h_out, q, [v.astype(jnp.bfloat16) for v in chunk(s.top_map, q)])
             h_copy(q).start()
 
     def part_copy(hop):
@@ -263,6 +282,9 @@
     @pl.when(last)
     def _():
         send_rows(TOP, -1, whole(s.top_map))
+        for c in range(9):
+            s.full_out[c] = s.top_map[c]
+        full_copy.start()
 
     send_rows(ENDS, 0, whole(s.end_map))
 
@@ -289,15 +311,23 @@
     def relay():
         for q in range(chunks):
             h_copy(q).wait_recv()
-            inner = mat_mat(whole(s.h_in.at[q]), chunk(s.end_map, q))
+            inner = mat_mat(h_part(q), chunk(s.end_map, q))
             value = added(chunk(s.top_map, q), mat_mat(chunk(s.top_map, q, 9), inner))
-            put(s.h_out, q, value)
+            put(s.h_out, q, [v.astype(jnp.bfloat16) for v in value])
             h_copy(q).start()
             for c in range(9):
                 s.row_out[TOP, 0, c : c + 1, q * LANES : (q + 1) * LANES] = value[c][R - 1 : R]
                 s.row_out[TOP, 1, c : c + 1, q * LANES : (q + 1) * LANES] = value[c][0:1]
         for side in range(2):
             row_copy(TOP, side, -1).start()
+
+    def full_relay():
+        full_copy.wait_recv()
+        inner = mat_mat(whole(s.full_in), whole(s.end_map))
+        outer = mat_mat([s.top_map[9 + c] for c in range(9)], inner)
+        for c in range(9):
+            s.full_out[c] = s.top_map[c] + outer[c]
+        full_copy.start()
 
     early = jnp.logical_and(inside, place == N - 2)
 
@@ -406,8 +436,9 @@
             ]
 
         def forward(k, state):
-            right = added(source(k), [link[k] * v for v in state])
-            state = mat_vec(planes(pivot, k, 9), right)
+            state = fold(
+                mat_vec(planes(pivot, k, 9), source(k)), planes(s.rise, k, 9), state
+            )
             put(values, k, state)
             return state
 
@@ -415,7 +446,7 @@
             planes(pivot, 0, 9), added(source(0), [wall[c] for c in range(3)])
         )
         put(values, 0, start)
-        ends = later(K, forward, start)
+        ends = later(K, forward, start, K - 1)
         if shared:
             put_rows(s.fe_out.at[sweep, 0], [v[R - 1 : R] for v in ends])
             put_rows(s.fe_out.at[sweep, 1], [v[0:1] for v in ends])
@@ -442,14 +473,12 @@
 
         def backward(step, state):
             k = K - 1 - step
-            state = added(
-                planes(values, k), mat_vec(planes(pivot, k, 9), [link[k + 1] * v for v in state])
-            )
+            state = fold(planes(values, k), planes(s.fall, k, 9), state)
             keep(k, state)
             return state
 
         keep(K - 1, ends)
-        tops = later(K, backward, ends)
+        tops = later(K, backward, ends, K - 1)
 
         if sweep == 0:
 
@@ -461,7 +490,7 @@
         def _():
             top = added(
                 [link[0] * v for v in tops],
-                mat_vec([s.top_map[9 + c] for c in range(9)], mat_vec(h_full(), ends)),
+                mat_vec([s.top_map[9 + c] for c in range(9)], mat_vec(h_full(sweep), ends)),
             )
             if shared:
                 put_rows(s.oe_out.at[sweep, 0], [v[R - 1 : R] for v in top])
@@ -487,6 +516,11 @@
                 up_edge(sweep, side, 0).start()
 
         if sweep == 0:
+
+            @pl.when(early)
+            def _():
+                full_relay()
+
             s.enter[...] = jnp.zeros(s.enter.shape, jnp.float32)
 
         for j in range(1, N):
@@ -516,16 +550,19 @@
                     moved = mat_vec(planes(s.down_in, j - 1, 9), moved)
                 put(s.enter, 1, added(planes(s.enter, 1), moved))
 
-        if sweep == 0:
+        if sweep < 2:
 
             @pl.when(first)
             def _():
-                for q in range(chunks):
-                    h_copy(q).wait_recv()
+                if sweep == 0:
+                    for q in range(chunks):
+                        h_copy(q).wait_recv()
+                else:
+                    full_copy.wait_recv()
 
         entering = planes(s.enter, 0)
         state = added(ends, mat_vec(whole(s.end_map), entering))
-        above = added(planes(s.enter, 1), mat_vec(h_full(), state))
+        above = added(planes(s.enter, 1), mat_vec(h_full(sweep), state))
 
         def finish(k, carry):
             state = added(planes(values, k), mat_vec(planes(maps, k, 9), entering))
@@ -534,6 +571,12 @@
             return carry
 
         loop(K, finish, 0, 4)
+
+        if sweep == 0:
+
+            @pl.when(jnp.logical_and(inside, jnp.logical_not(early)))
+            def _():
+                full_relay()
 
         if shared:
             if sweep == 0:
@@ -609,6 +652,7 @@
 
     @pl.when(jnp.logical_not(first))
     def _():
+        full_copy.wait_send()
         for q in range(chunks):
             h_copy(q).wait_send()
         for side in range(2):
@@ -678,6 +722,8 @@
         pivot=room(K, 9, R, W),
         stiffness=room(K, R, W),
         link=room(K, R, W),
+        rise=room(K, 9, R, W),
+        fall=room(K, 9, R, W),
         maps=room(K, 18, R, W),
         end_map=room(9, R, W),
         top_map=room(18, R, W),
@@ -706,8 +752,10 @@
         fe_out=room(G, 2, 3, W),
         oe_in=room(G, 2, N, 3, W),
         oe_out=room(G, 2, 3, W),
-        h_in=room(C, 9, R, LANES),
-        h_out=room(C, 9, R, LANES),
+        h_in=half(C, 9, R, LANES),
+        h_out=half(C, 9, R, LANES),
+        full_in=room(9, R, W),
+        full_out=room(9, R, W),
         up_in=room(N, 9, R, W),
         up_out=room(N, 9, R, W),
         down_in=room(N, 9, R, W),
@@ -715,12 +763,12 @@
         load_sem=dma((3 + modes.shape[2] // (2 * R),)),
     )
     sems = dict(
-        part=(S,), mask=(2,), h=(C,), row=(2 * N, 2), side=(2,), up=(N,), down=(N,),
+        part=(S,), mask=(2,), h=(C,), full=(), row=(2 * N, 2), side=(2,), up=(N,), down=(N,),
         f=(SWEEPS, N), o=(SWEEPS, N), fe=(G, 2, N), oe=(G, 2, N), edge=(G, 2),
     )
     for name, shape in sems.items():
-        scratch[name + "_send"] = dma(shape)
-        scratch[name + "_recv"] = dma(shape)
+        scratch[name + "_send"] = dma(shape) if shape else dma
+        scratch[name + "_recv"] = dma(shape) if shape else dma
     out = pl.pallas_call(
         functools.partial(kernel, S, N, tuple(scratch)),
         out_shape=pltpu.VMEM((K, 3, R, W), f32),

time: 31.3 us -> 30.3 us (0.968)
  Pallas kernels: 30.4 us -> 29.4 us
    pallas_call x1, Pallas kernels: 30.4 us -> 29.4 us  [per_device(): pl.pallas_call(functools.partial(kernel, S, N, tuple(scratch)), out_shape...]
where the time goes in v4:
time: 30.3 us; the launch traced here: 30.1 us
  Pallas kernels  29.4 us (97%)
  local copies, waits for them, and re-layouts  0.75 us (2%)
    pallas_call x1, Pallas kernels, per_device(): pl.pallas_call(functools.partial(kernel, S, N, tuple(scratch)), out_shape...  29.4 us
    unnamed x1, local copies, waits for them, and re-layouts  0.75 us

profile of v4, /device:TPU:0, one launch (start us, length us, event | category | flops | bytes accessed | tf_op | source)
XLA Modules:
  0.0 30.1 jit_solution(17654150637491369753)
XLA Ops:
  0.0 29.4 %line_sweeps.1 = f32[16,3,8,256]{3,2,1,0:T(8,128)S(1)} custom-call(f32[128]{0:T(128)} %amplitude.1, s32[128]{0:T(128)} %mode_patch.1, s32[64,256]{1,0:T(8,128)} %column_patch.1, s32[8,256]{1,0:T(8,128)} %wall_mask.1, s32[8,256]{1,0:T(8,128)} %offsets.1, bf16[16,3,64,256]{3,2,1,0:T(8,128)(2,1)} %bitcast.4, f32[16,8,256]{2,1,0:T(8,128)} %coupling_hbm.1, ...), custom_call_target="tpu_custom_call" | custom-call | tf_op jit(solution)/shard_map/line_sweeps/pallas_call | solution.py:772
  29.4 0.7 %copy.11 = f32[16,8,3,256]{3,1,2,0:T(8,128)} copy(f32[16,8,3,256]{3,1,2,0:T(8,128)S(1)} %bitcast.3) | data formatting | bytes 786432

commit v5 on v4

--- a/solution.py
+++ b/solution.py
@@ -110,6 +110,9 @@
     def toward(side):
         return after if side == 0 else before
 
+    def settle(ref, sem):
+        pltpu.make_async_copy(ref, ref, sem).wait()
+
     mode_loads = [
         pltpu.make_async_copy(
             modes_hbm.at[:, :, pl.ds(b * B, B), :], modes.at[:, :, pl.ds(b * B, B), :], s.load_sem.at[3 + b]
@@ -219,7 +222,7 @@
     def row_copy(slot, side, step):
         return to(
             s.row_out.at[slot, side], s.row_in.at[slot, side],
-            s.row_send.at[slot, side], s.row_recv.at[slot, side],
+            s.row_send.at[slot], s.row_recv.at[slot],
             surf=toward(side), norm=place + step,
         )
 
@@ -229,13 +232,13 @@
         for side in range(2):
             row_copy(slot, side, step).start()
 
-    UP, DOWN, ENDS, TOP = 0, N, 0, N
+    UP, DOWN, ENDS, TOP = 0, N - 1, 0, N - 1
 
     def up_map(j):
-        return to(s.up_out.at[j], s.up_in.at[j], s.up_send.at[j], s.up_recv.at[j], norm=place + 1)
+        return to(s.up_out.at[j], s.up_in.at[j], s.up_send.at[j - 1], s.up_recv.at[j - 1], norm=place + 1)
 
     def down_map(j):
-        return to(s.down_out.at[j], s.down_in.at[j], s.down_send.at[j], s.down_recv.at[j], norm=place - 1)
+        return to(s.down_out.at[j], s.down_in.at[j], s.down_send.at[j - 1], s.down_recv.at[j - 1], norm=place - 1)
 
     def sends_up(j):
         return jnp.logical_and(place >= j, jnp.logical_not(last))
@@ -254,12 +257,12 @@
 
     def part_copy(hop):
         dest = lax.rem(me + hop, S)
-        return to(part.at[dest], got.at[hop], s.part_send.at[hop], s.part_recv.at[hop], surf=dest)
+        return to(part.at[dest], got.at[hop], s.part_send, s.part_recv, surf=dest)
 
     for hop in range(1, S):
         part_copy(hop).start()
-    mask_up = to(wall_mask, s.mask_edge.at[0], s.mask_send.at[0], s.mask_recv.at[0], surf=after)
-    mask_down = to(wall_mask, s.mask_edge.at[1], s.mask_send.at[1], s.mask_recv.at[1], surf=before)
+    mask_up = to(wall_mask, s.mask_edge.at[0], s.mask_send, s.mask_recv, surf=after)
+    mask_down = to(wall_mask, s.mask_edge.at[1], s.mask_send, s.mask_recv, surf=before)
     mask_up.start()
     mask_down.start()
 
@@ -299,7 +302,7 @@
 
     def side_map_copy(side):
         return to(
-            s.side_out.at[side], s.side_in.at[side], s.side_send.at[side], s.side_recv.at[side],
+            s.side_out.at[side], s.side_in.at[side], s.side_send, s.side_recv,
             surf=toward(side),
         )
 
@@ -354,10 +357,9 @@
             send_rows(DOWN + j, -1, value)
 
     total = [part[me, c] for c in range(4)]
-    mask_up.wait_recv()
-    mask_down.wait_recv()
+    settle(s.mask_edge, s.mask_recv)
+    settle(got.at[pl.ds(0, S - 1)], s.part_recv)
     for hop in range(1, S):
-        part_copy(hop).wait_recv()
         total = [total[c] + got[hop, c] for c in range(4)]
     mask = wall_mask[...].astype(jnp.float32)
     low_mask = s.mask_edge[0, R - 1 : R, :].astype(jnp.float32)
@@ -382,32 +384,32 @@
     def edge_copy(sweep, side):
         return to(
             s.edge_out.at[sweep, side], s.edge_in.at[sweep, side],
-            s.edge_send.at[sweep, side], s.edge_recv.at[sweep, side], surf=toward(side),
+            s.edge_send.at[sweep], s.edge_recv.at[sweep], surf=toward(side),
         )
 
     def up_copy(sweep, j):
         return to(
-            s.f_out.at[sweep], s.f_in.at[sweep, j], s.f_send.at[sweep, j], s.f_recv.at[sweep, j],
+            s.f_out.at[sweep], s.z_in.at[sweep, place], s.z_send.at[sweep], s.z_recv.at[sweep],
             norm=place + j,
         )
 
     def down_copy(sweep, j):
         return to(
-            s.o_out.at[sweep], s.o_in.at[sweep, j], s.o_send.at[sweep, j], s.o_recv.at[sweep, j],
+            s.o_out.at[sweep], s.z_in.at[sweep, place], s.z_send.at[sweep], s.z_recv.at[sweep],
             norm=place - j,
         )
 
     def up_edge(sweep, side, j):
         return to(
-            s.fe_out.at[sweep, side], s.fe_in.at[sweep, side, j],
-            s.fe_send.at[sweep, side, j], s.fe_recv.at[sweep, side, j],
+            s.fe_out.at[sweep, side], s.e_in.at[sweep, side, place],
+            s.e_send.at[sweep], s.e_recv.at[sweep],
             surf=toward(side), norm=place + j,
         )
 
     def down_edge(sweep, side, j):
         return to(
-            s.oe_out.at[sweep, side], s.oe_in.at[sweep, side, j],
-            s.oe_send.at[sweep, side, j], s.oe_recv.at[sweep, side, j],
+            s.oe_out.at[sweep, side], s.e_in.at[sweep, side, place],
+            s.e_send.at[sweep], s.e_recv.at[sweep],
             surf=toward(side), norm=place - j,
         )
 
@@ -523,6 +525,7 @@
 
             s.enter[...] = jnp.zeros(s.enter.shape, jnp.float32)
 
+        settle(s.z_in.at[sweep, pl.ds(0, N - 1)], s.z_recv.at[sweep])
         for j in range(1, N):
             if sweep == 0 and j > 1:
 
@@ -536,16 +539,14 @@
 
             @pl.when(place - j >= 0)
             def _():
-                up_copy(sweep, j).wait_recv()
-                moved = wide(s.f_in.at[sweep], j)
+                moved = wide(s.z_in.at[sweep], place - j)
                 if j > 1:
                     moved = mat_vec(planes(s.up_in, j - 1, 9), moved)
                 put(s.enter, 0, added(planes(s.enter, 0), moved))
 
             @pl.when(place + j < N)
             def _():
-                down_copy(sweep, j).wait_recv()
-                moved = wide(s.o_in.at[sweep], j)
+                moved = wide(s.z_in.at[sweep], place + j)
                 if j > 1:
                     moved = mat_vec(planes(s.down_in, j - 1, 9), moved)
                 put(s.enter, 1, added(planes(s.enter, 1), moved))
@@ -580,35 +581,32 @@
 
         if shared:
             if sweep == 0:
-                for side in range(2):
-                    side_map_copy(side).wait_recv()
-                    row_copy(ENDS, side, 0).wait_recv()
+                settle(s.side_in, s.side_recv)
+                settle(s.row_in.at[ENDS], s.row_recv.at[ENDS])
 
                 @pl.when(jnp.logical_not(last))
                 def _():
-                    for side in range(2):
-                        row_copy(TOP, side, 0).wait_recv()
+                    settle(s.row_in.at[TOP], s.row_recv.at[TOP])
 
                 for j in range(2, N):
 
                     @pl.when(place >= j)
                     def _():
-                        for side in range(2):
-                            row_copy(UP + j - 1, side, 0).wait_recv()
+                        settle(s.row_in.at[UP + j - 1], s.row_recv.at[UP + j - 1])
 
                     @pl.when(N - 1 - place >= j)
                     def _():
-                        for side in range(2):
-                            row_copy(DOWN + j - 1, side, 0).wait_recv()
-
+                        settle(s.row_in.at[DOWN + j - 1], s.row_recv.at[DOWN + j - 1])
+
+            settle(s.e_in.at[sweep], s.e_recv.at[sweep])
+            settle(s.edge_in.at[sweep], s.edge_recv.at[sweep])
             s.enter_row[...] = jnp.zeros(s.enter_row.shape, jnp.float32)
             for j in range(1, N):
 
                 @pl.when(place - j >= 0)
                 def _():
                     for side in range(2):
-                        up_edge(sweep, side, j).wait_recv()
-                        moved = rows(s.fe_in.at[sweep, side, j])
+                        moved = rows(s.e_in.at[sweep, side, place - j])
                         if j > 1:
                             moved = mat_vec(rows(s.row_in.at[UP + j - 1, side], 9), moved)
                         put_rows(s.enter_row.at[side, 0], added(rows(s.enter_row.at[side, 0]), moved))
@@ -616,18 +614,15 @@
                 @pl.when(place + j < N)
                 def _():
                     for side in range(2):
-                        down_edge(sweep, side, j).wait_recv()
-                        moved = rows(s.oe_in.at[sweep, side, j])
+                        moved = rows(s.e_in.at[sweep, side, place + j])
                         if j > 1:
                             moved = mat_vec(rows(s.row_in.at[DOWN + j - 1, side], 9), moved)
                         put_rows(s.enter_row.at[side, 1], added(rows(s.enter_row.at[side, 1]), moved))
 
             for side in range(2):
-                up_edge(sweep, side, 0).wait_recv()
-                edge_copy(sweep, side).wait_recv()
                 entered = rows(s.enter_row.at[side, 0])
                 state = added(
-                    rows(s.fe_in.at[sweep, side, 0]),
+                    rows(s.e_in.at[sweep, side, place]),
                     mat_vec(rows(s.row_in.at[ENDS, side], 9), entered),
                 )
                 higher = added(
@@ -640,58 +635,34 @@
                         value += s.side_in[side, 9 + 3 * c + b].astype(jnp.float32) * higher[b]
                     halo[side, c] = value
 
-    for hop in range(1, S):
-        part_copy(hop).wait_send()
-    mask_up.wait_send()
-    mask_down.wait_send()
-    for side in range(2):
-        side_map_copy(side).wait_send()
-        row_copy(ENDS, side, 0).wait_send()
-        for sweep in range(SWEEPS - 1):
-            edge_copy(sweep, side).wait_send()
+    settle(got.at[pl.ds(0, S - 1)], s.part_send)
+    settle(s.mask_edge, s.mask_send)
+    settle(s.side_out, s.side_send)
+    settle(s.row_out.at[ENDS], s.row_send.at[ENDS])
+    for sweep in range(SWEEPS):
+        settle(s.z_in.at[sweep, pl.ds(0, N - 1)], s.z_send.at[sweep])
+    for sweep in range(SWEEPS - 1):
+        settle(s.edge_out.at[sweep], s.edge_send.at[sweep])
+        settle(s.e_in.at[sweep], s.e_send.at[sweep])
 
     @pl.when(jnp.logical_not(first))
     def _():
         full_copy.wait_send()
         for q in range(chunks):
             h_copy(q).wait_send()
-        for side in range(2):
-            row_copy(TOP, side, 0).wait_send()
+        settle(s.row_out.at[TOP], s.row_send.at[TOP])
 
     for j in range(1, N - 1):
 
         @pl.when(sends_up(j))
         def _():
             up_map(j).wait_send()
-            for side in range(2):
-                row_copy(UP + j, side, 0).wait_send()
+            settle(s.row_out.at[UP + j], s.row_send.at[UP + j])
 
         @pl.when(sends_down(j))
         def _():
             down_map(j).wait_send()
-            for side in range(2):
-                row_copy(DOWN + j, side, 0).wait_send()
-
-    for j in range(N):
-
-        @pl.when(place + j < N)
-        def _():
-            for sweep in range(SWEEPS):
-                if j > 0:
-                    up_copy(sweep, j).wait_send()
-                if sweep < SWEEPS - 1:
-                    for side in range(2):
-                        up_edge(sweep, side, j).wait_send()
-
-        if j > 0:
-
-            @pl.when(place - j >= 0)
-            def _():
-                for sweep in range(SWEEPS):
-                    down_copy(sweep, j).wait_send()
-                    if sweep < SWEEPS - 1:
-                        for side in range(2):
-                            down_edge(sweep, side, j).wait_send()
+            settle(s.row_out.at[DOWN + j], s.row_send.at[DOWN + j])
 
 
 def per_device(
@@ -740,17 +711,15 @@
         side_rows=room(2, 18, K, W),
         side_out=half(2, 18, K, W),
         side_in=half(2, 18, K, W),
-        row_out=room(2 * N, 2, 9, W),
-        row_in=room(2 * N, 2, 9, W),
-        f_in=half(SWEEPS, N, 3, R, W),
+        row_out=room(2 * N - 2, 2, 9, W),
+        row_in=room(2 * N - 2, 2, 9, W),
+        z_in=half(SWEEPS, N, 3, R, W),
         f_out=half(SWEEPS, 3, R, W),
         f_sent=room(3, R, W),
-        o_in=half(SWEEPS, N, 3, R, W),
         o_out=half(SWEEPS, 3, R, W),
         o_sent=room(3, R, W),
-        fe_in=room(G, 2, N, 3, W),
+        e_in=room(G, 2, N, 3, W),
         fe_out=room(G, 2, 3, W),
-        oe_in=room(G, 2, N, 3, W),
         oe_out=room(G, 2, 3, W),
         h_in=half(C, 9, R, LANES),
         h_out=half(C, 9, R, LANES),
@@ -763,8 +732,8 @@
         load_sem=dma((3 + modes.shape[2] // (2 * R),)),
     )
     sems = dict(
-        part=(S,), mask=(2,), h=(C,), full=(), row=(2 * N, 2), side=(2,), up=(N,), down=(N,),
-        f=(SWEEPS, N), o=(SWEEPS, N), fe=(G, 2, N), oe=(G, 2, N), edge=(G, 2),
+        part=(), mask=(), h=(C,), full=(), row=(2 * N - 2,), side=(), up=(max(N - 2, 1),),
+        down=(max(N - 2, 1),), z=(SWEEPS,), e=(G,), edge=(G,),
     )
     for name, shape in sems.items():
         scratch[name + "_send"] = dma(shape) if shape else dma

time: 30.3 us -> 28.9 us (0.954)
  Pallas kernels: 29.4 us -> 27.9 us
    pallas_call x1, Pallas kernels: 29.4 us -> 27.9 us  [per_device(): pl.pallas_call(functools.partial(kernel, S, N, tuple(scratch)), out_shape...]
where the time goes in v5:
time: 28.9 us; the launch traced here: 28.7 us
  Pallas kernels  27.9 us (97%)
  local copies, waits for them, and re-layouts  0.75 us (3%)
    pallas_call x1, Pallas kernels, per_device(): pl.pallas_call(functools.partial(kernel, S, N, tuple(scratch)), out_shape...  27.9 us
    unnamed x1, local copies, waits for them, and re-layouts  0.75 us

profile of v5, /device:TPU:0, one launch (start us, length us, event | category | flops | bytes accessed | tf_op | source)
XLA Modules:
  0.0 28.7 jit_solution(8070577844142101694)
XLA Ops:
  0.0 27.9 %line_sweeps.1 = f32[16,3,8,256]{3,2,1,0:T(8,128)S(1)} custom-call(f32[128]{0:T(128)} %amplitude.1, s32[128]{0:T(128)} %mode_patch.1, s32[64,256]{1,0:T(8,128)} %column_patch.1, s32[8,256]{1,0:T(8,128)} %wall_mask.1, s32[8,256]{1,0:T(8,128)} %offsets.1, bf16[16,3,64,256]{3,2,1,0:T(8,128)(2,1)} %bitcast.4, f32[16,8,256]{2,1,0:T(8,128)} %coupling_hbm.1, ...), custom_call_target="tpu_custom_call" | custom-call | tf_op jit(solution)/shard_map/line_sweeps/pallas_call | solution.py:741
  27.9 0.7 %copy.11 = f32[16,8,3,256]{3,1,2,0:T(8,128)} copy(f32[16,8,3,256]{3,1,2,0:T(8,128)S(1)} %bitcast.3) | data formatting | bytes 786432

commit v6 on v5

--- a/solution.py
+++ b/solution.py
@@ -80,12 +80,14 @@
 
 def kernel(
     surf_size, norm_size, names,
-    amplitude, mode_patch, column_patch, wall_mask, offsets,
+    amplitude_hbm, mode_patch_hbm, column_patch_hbm, wall_mask_hbm, offsets_hbm,
     modes_hbm, coupling_hbm, pivot_hbm, stiffness_hbm,
     out, *scratch,
 ):
     s = types.SimpleNamespace(**dict(zip(names, scratch)))
     modes, coupling, pivot, stiffness = s.modes, s.coupling, s.pivot, s.stiffness
+    amplitude, mode_patch, column_patch = s.amplitude, s.mode_patch, s.column_patch
+    wall_mask, offsets = s.wall_mask, s.offsets
     link, maps, part, got, wall, values, halo = s.link, s.maps, s.part, s.got, s.wall, s.values, s.halo
     S, N = surf_size, norm_size
     K, _, R, W = pivot.shape
@@ -113,18 +115,20 @@
     def settle(ref, sem):
         pltpu.make_async_copy(ref, ref, sem).wait()
 
+    line_loads = [
+        pltpu.make_async_copy(src, dst, s.load_sem.at[index])
+        for index, (src, dst) in enumerate([
+            (pivot_hbm, pivot), (coupling_hbm, coupling), (offsets_hbm, offsets),
+        ])
+    ]
     mode_loads = [
-        pltpu.make_async_copy(
-            modes_hbm.at[:, :, pl.ds(b * B, B), :], modes.at[:, :, pl.ds(b * B, B), :], s.load_sem.at[3 + b]
-        )
-        for b in range(blocks)
+        pltpu.make_async_copy(src, dst, s.load_sem.at[3 + index])
+        for index, (src, dst) in enumerate([
+            (modes_hbm, modes), (column_patch_hbm, column_patch), (amplitude_hbm, amplitude),
+            (mode_patch_hbm, mode_patch), (wall_mask_hbm, wall_mask), (stiffness_hbm, stiffness),
+        ])
     ]
-    loads = [
-        pltpu.make_async_copy(coupling_hbm, coupling, s.load_sem.at[0]),
-        pltpu.make_async_copy(pivot_hbm, pivot, s.load_sem.at[1]),
-        pltpu.make_async_copy(stiffness_hbm, stiffness, s.load_sem.at[2]),
-    ]
-    for copy in loads + mode_loads:
+    for copy in line_loads + mode_loads:
         copy.start()
 
     barrier = pltpu.get_barrier_semaphore()
@@ -140,7 +144,7 @@
         greet(surf=before, norm=other)
         greet(surf=after, norm=other)
 
-    for copy in loads:
+    for copy in line_loads:
         copy.wait()
     cut = offsets[...]
 
@@ -177,9 +181,10 @@
     for c in range(18):
         s.top_map[c] = link[0] * top_state[c]
 
+    for copy in mode_loads:
+        copy.wait()
     own_mode = me * M
     for b in range(blocks):
-        mode_loads[b].wait()
         patch = column_patch[b * B : (b + 1) * B, :]
 
         def mode_step(m, sums):
@@ -384,32 +389,32 @@
     def edge_copy(sweep, side):
         return to(
             s.edge_out.at[sweep, side], s.edge_in.at[sweep, side],
-            s.edge_send.at[sweep], s.edge_recv.at[sweep], surf=toward(side),
+            s.edge_send, s.edge_recv.at[sweep], surf=toward(side),
         )
 
     def up_copy(sweep, j):
         return to(
-            s.f_out.at[sweep], s.z_in.at[sweep, place], s.z_send.at[sweep], s.z_recv.at[sweep],
+            s.f_out.at[sweep], s.z_in.at[sweep, place], s.z_send, s.z_recv.at[sweep],
             norm=place + j,
         )
 
     def down_copy(sweep, j):
         return to(
-            s.o_out.at[sweep], s.z_in.at[sweep, place], s.z_send.at[sweep], s.z_recv.at[sweep],
+            s.o_out.at[sweep], s.z_in.at[sweep, place], s.z_send, s.z_recv.at[sweep],
             norm=place - j,
         )
 
     def up_edge(sweep, side, j):
         return to(
             s.fe_out.at[sweep, side], s.e_in.at[sweep, side, place],
-            s.e_send.at[sweep], s.e_recv.at[sweep],
+            s.e_send, s.e_recv.at[sweep],
             surf=toward(side), norm=place + j,
         )
 
     def down_edge(sweep, side, j):
         return to(
             s.oe_out.at[sweep, side], s.e_in.at[sweep, side, place],
-            s.e_send.at[sweep], s.e_recv.at[sweep],
+            s.e_send, s.e_recv.at[sweep],
             surf=toward(side), norm=place - j,
         )
 
@@ -571,7 +576,7 @@
             put(out, k, state)
             return carry
 
-        loop(K, finish, 0, 4)
+        loop(K, finish, 0, 8)
 
         if sweep == 0:
 
@@ -639,11 +644,9 @@
     settle(s.mask_edge, s.mask_send)
     settle(s.side_out, s.side_send)
     settle(s.row_out.at[ENDS], s.row_send.at[ENDS])
-    for sweep in range(SWEEPS):
-        settle(s.z_in.at[sweep, pl.ds(0, N - 1)], s.z_send.at[sweep])
-    for sweep in range(SWEEPS - 1):
-        settle(s.edge_out.at[sweep], s.edge_send.at[sweep])
-        settle(s.e_in.at[sweep], s.e_send.at[sweep])
+    settle(s.z_in.at[:, pl.ds(0, N - 1)], s.z_send)
+    settle(s.edge_out, s.edge_send)
+    settle(s.e_in, s.e_send)
 
     @pl.when(jnp.logical_not(first))
     def _():
@@ -676,7 +679,6 @@
     C = W // LANES
     f32, bf16 = jnp.float32, jnp.bfloat16
     vmem = pl.BlockSpec(memory_space=pltpu.VMEM)
-    smem = pl.BlockSpec(memory_space=pltpu.SMEM)
     hbm = pl.BlockSpec(memory_space=pltpu.HBM)
     dma = pltpu.SemaphoreType.DMA
 
@@ -729,19 +731,24 @@
         up_out=room(N, 9, R, W),
         down_in=room(N, 9, R, W),
         down_out=room(N, 9, R, W),
-        load_sem=dma((3 + modes.shape[2] // (2 * R),)),
+        load_sem=dma((9,)),
+        amplitude=pltpu.SMEM(amplitude.shape, f32),
+        mode_patch=pltpu.SMEM(mode_patch.shape, jnp.int32),
+        column_patch=pltpu.VMEM(column_patch.shape, jnp.int32),
+        wall_mask=pltpu.VMEM(wall_mask.shape, jnp.int32),
+        offsets=pltpu.VMEM(offsets.shape, jnp.int32),
     )
     sems = dict(
         part=(), mask=(), h=(C,), full=(), row=(2 * N - 2,), side=(), up=(max(N - 2, 1),),
         down=(max(N - 2, 1),), z=(SWEEPS,), e=(G,), edge=(G,),
     )
     for name, shape in sems.items():
-        scratch[name + "_send"] = dma(shape) if shape else dma
+        scratch[name + "_send"] = dma(shape) if shape and name not in ("z", "e", "edge") else dma
         scratch[name + "_recv"] = dma(shape) if shape else dma
     out = pl.pallas_call(
         functools.partial(kernel, S, N, tuple(scratch)),
         out_shape=pltpu.VMEM((K, 3, R, W), f32),
-        in_specs=[smem, smem, vmem, vmem, vmem, hbm, hbm, hbm, hbm],
+        in_specs=[hbm] * 9,
         out_specs=vmem,
         scratch_shapes=list(scratch.values()),
         compiler_params=pltpu.CompilerParams(

time: 28.9 us -> 27.9 us (0.965)
  Pallas kernels: 27.9 us -> 27 us
    pallas_call x1, Pallas kernels: 27.9 us -> 27 us  [per_device(): pl.pallas_call(functools.partial(kernel, S, N, tuple(scratch)), out_shape...]
where the time goes in v6:
time: 27.9 us; the launch traced here: 27.7 us
  Pallas kernels  27 us (97%)
  local copies, waits for them, and re-layouts  0.75 us (3%)
    pallas_call x1, Pallas kernels, per_device(): pl.pallas_call(functools.partial(kernel, S, N, tuple(scratch)), out_shape...  27 us
    unnamed x1, local copies, waits for them, and re-layouts  0.75 us

profile of v6, /device:TPU:0, one launch (start us, length us, event | category | flops | bytes accessed | tf_op | source)
XLA Modules:
  0.0 27.7 jit_solution(2692184148101005706)
XLA Ops:
  0.0 27.0 %line_sweeps.1 = f32[16,3,8,256]{3,2,1,0:T(8,128)S(1)} custom-call(f32[128]{0:T(128)} %amplitude_hbm.1, s32[128]{0:T(128)} %mode_patch_hbm.1, s32[64,256]{1,0:T(8,128)} %column_patch_hbm.1, s32[8,256]{1,0:T(8,128)} %wall_mask_hbm.1, s32[8,256]{1,0:T(8,128)} %offsets_hbm.1, bf16[16,3,64,256]{3,2,1,0:T(8,128)(2,1)} %bitcast.4, f32[16,8,256]{2,1,0:T(8,128)} %coupling_hbm.1, ...), custom_call_target="tpu_custom_call" | custom-call | tf_op jit(solution)/shard_map/line_sweeps/pallas_call | solution.py:748
  27.0 0.7 %copy.11 = f32[16,8,3,256]{3,1,2,0:T(8,128)} copy(f32[16,8,3,256]{3,1,2,0:T(8,128)S(1)} %bitcast.3) | data formatting | bytes 786432

commit v7 on v6

--- a/solution.py
+++ b/solution.py
@@ -251,6 +251,17 @@
     def sends_down(j):
         return jnp.logical_and(N - 1 - place >= j, jnp.logical_not(first))
 
+    def part_copy(hop):
+        dest = lax.rem(me + hop, S)
+        return to(part.at[dest], got.at[hop], s.part_send, s.part_recv, surf=dest)
+
+    for hop in range(1, S):
+        part_copy(hop).start()
+    mask_up = to(wall_mask, s.mask_edge.at[0], s.mask_send, s.mask_recv, surf=after)
+    mask_down = to(wall_mask, s.mask_edge.at[1], s.mask_send, s.mask_recv, surf=before)
+    mask_up.start()
+    mask_down.start()
+
     @pl.when(last)
     def _():
         s.h_in[...] = jnp.zeros(s.h_in.shape, jnp.bfloat16)
@@ -260,17 +271,6 @@
             put(s.h_out, q, [v.astype(jnp.bfloat16) for v in chunk(s.top_map, q)])
             h_copy(q).start()
 
-    def part_copy(hop):
-        dest = lax.rem(me + hop, S)
-        return to(part.at[dest], got.at[hop], s.part_send, s.part_recv, surf=dest)
-
-    for hop in range(1, S):
-        part_copy(hop).start()
-    mask_up = to(wall_mask, s.mask_edge.at[0], s.mask_send, s.mask_recv, surf=after)
-    mask_down = to(wall_mask, s.mask_edge.at[1], s.mask_send, s.mask_recv, surf=before)
-    mask_up.start()
-    mask_down.start()
-
     for j in range(1, min(2, N - 1)):
 
         @pl.when(sends_up(j))
@@ -295,26 +295,6 @@
         full_copy.start()
 
     send_rows(ENDS, 0, whole(s.end_map))
-
-    def pack_step(k, carry):
-        for c in range(18):
-            value = maps[k, c]
-            s.side_rows[0, c, pl.ds(k, 1), :] = value[R - 1 : R]
-            s.side_rows[1, c, pl.ds(k, 1), :] = value[0:1]
-        return carry
-
-    loop(K, pack_step, 0, 2)
-
-    def side_map_copy(side):
-        return to(
-            s.side_out.at[side], s.side_in.at[side], s.side_send, s.side_recv,
-            surf=toward(side),
-        )
-
-    for side in range(2):
-        for c in range(18):
-            s.side_out[side, c] = s.side_rows[side, c].astype(jnp.bfloat16)
-        side_map_copy(side).start()
 
     def relay():
         for q in range(chunks):
@@ -361,6 +341,26 @@
             down_map(j).start()
             send_rows(DOWN + j, -1, value)
 
+    def pack_step(k, carry):
+        for c in range(18):
+            value = maps[k, c]
+            s.side_rows[0, c, pl.ds(k, 1), :] = value[R - 1 : R]
+            s.side_rows[1, c, pl.ds(k, 1), :] = value[0:1]
+        return carry
+
+    loop(K, pack_step, 0, 2)
+
+    def side_map_copy(side):
+        return to(
+            s.side_out.at[side], s.side_in.at[side], s.side_send, s.side_recv,
+            surf=toward(side),
+        )
+
+    for side in range(2):
+        for c in range(18):
+            s.side_out[side, c] = s.side_rows[side, c].astype(jnp.bfloat16)
+        side_map_copy(side).start()
+
     total = [part[me, c] for c in range(4)]
     settle(s.mask_edge, s.mask_recv)
     settle(got.at[pl.ds(0, S - 1)], s.part_recv)
@@ -425,6 +425,15 @@
             send[sweep, c] = step
             sent[c] = known + step.astype(jnp.float32)
 
+    def lower_place(j):
+        return jnp.maximum(place - j, 0)
+
+    def upper_place(j):
+        return jnp.minimum(place + j, N - 1)
+
+    def only(valid, values3):
+        return [lax.select(valid, v, jnp.zeros_like(v)) for v in values3]
+
     def wide(ref, index):
         return [v.astype(jnp.float32) for v in planes(ref, index)]
 
@@ -528,7 +537,6 @@
             def _():
                 full_relay()
 
-            s.enter[...] = jnp.zeros(s.enter.shape, jnp.float32)
 
         settle(s.z_in.at[sweep, pl.ds(0, N - 1)], s.z_recv.at[sweep])
         for j in range(1, N):
@@ -542,19 +550,19 @@
                 def _():
                     down_map(j - 1).wait_recv()
 
-            @pl.when(place - j >= 0)
-            def _():
-                moved = wide(s.z_in.at[sweep], place - j)
-                if j > 1:
-                    moved = mat_vec(planes(s.up_in, j - 1, 9), moved)
-                put(s.enter, 0, added(planes(s.enter, 0), moved))
-
-            @pl.when(place + j < N)
-            def _():
-                moved = wide(s.z_in.at[sweep], place + j)
-                if j > 1:
-                    moved = mat_vec(planes(s.down_in, j - 1, 9), moved)
-                put(s.enter, 1, added(planes(s.enter, 1), moved))
+        rising = planes(s.enter, 0) if sweep > 0 else [jnp.zeros((R, W), jnp.float32)] * 3
+        falling = planes(s.enter, 1) if sweep > 0 else [jnp.zeros((R, W), jnp.float32)] * 3
+        for j in range(1, N):
+            moved = wide(s.z_in.at[sweep], lower_place(j))
+            if j > 1:
+                moved = mat_vec(planes(s.up_in, j - 1, 9), moved)
+            rising = added(rising, only(place >= j, moved))
+            moved = wide(s.z_in.at[sweep], upper_place(j))
+            if j > 1:
+                moved = mat_vec(planes(s.down_in, j - 1, 9), moved)
+            falling = added(falling, only(place + j < N, moved))
+        put(s.enter, 0, rising)
+        put(s.enter, 1, falling)
 
         if sweep < 2:
 
@@ -566,9 +574,9 @@
                 else:
                     full_copy.wait_recv()
 
-        entering = planes(s.enter, 0)
+        entering = rising
         state = added(ends, mat_vec(whole(s.end_map), entering))
-        above = added(planes(s.enter, 1), mat_vec(h_full(sweep), state))
+        above = added(falling, mat_vec(h_full(sweep), state))
 
         def finish(k, carry):
             state = added(planes(values, k), mat_vec(planes(maps, k, 9), entering))
@@ -605,33 +613,24 @@
 
             settle(s.e_in.at[sweep], s.e_recv.at[sweep])
             settle(s.edge_in.at[sweep], s.edge_recv.at[sweep])
-            s.enter_row[...] = jnp.zeros(s.enter_row.shape, jnp.float32)
-            for j in range(1, N):
-
-                @pl.when(place - j >= 0)
-                def _():
-                    for side in range(2):
-                        moved = rows(s.e_in.at[sweep, side, place - j])
-                        if j > 1:
-                            moved = mat_vec(rows(s.row_in.at[UP + j - 1, side], 9), moved)
-                        put_rows(s.enter_row.at[side, 0], added(rows(s.enter_row.at[side, 0]), moved))
-
-                @pl.when(place + j < N)
-                def _():
-                    for side in range(2):
-                        moved = rows(s.e_in.at[sweep, side, place + j])
-                        if j > 1:
-                            moved = mat_vec(rows(s.row_in.at[DOWN + j - 1, side], 9), moved)
-                        put_rows(s.enter_row.at[side, 1], added(rows(s.enter_row.at[side, 1]), moved))
-
             for side in range(2):
-                entered = rows(s.enter_row.at[side, 0])
+                entered = [jnp.zeros((1, W), jnp.float32)] * 3
+                leaving = [jnp.zeros((1, W), jnp.float32)] * 3
+                for j in range(1, N):
+                    moved = rows(s.e_in.at[sweep, side, lower_place(j)])
+                    if j > 1:
+                        moved = mat_vec(rows(s.row_in.at[UP + j - 1, side], 9), moved)
+                    entered = added(entered, only(place >= j, moved))
+                    moved = rows(s.e_in.at[sweep, side, upper_place(j)])
+                    if j > 1:
+                        moved = mat_vec(rows(s.row_in.at[DOWN + j - 1, side], 9), moved)
+                    leaving = added(leaving, only(place + j < N, moved))
                 state = added(
                     rows(s.e_in.at[sweep, side, place]),
                     mat_vec(rows(s.row_in.at[ENDS, side], 9), entered),
                 )
                 higher = added(
-                    rows(s.enter_row.at[side, 1]), mat_vec(rows(s.row_in.at[TOP, side], 9), state)
+                    leaving, mat_vec(rows(s.row_in.at[TOP, side], 9), state)
                 )
                 for c in range(3):
                     value = s.edge_in[sweep, side, c].astype(jnp.float32)
@@ -706,7 +705,6 @@
         wall=room(6, R, W),
         values=room(K, 3, R, W),
         enter=room(2, 3, R, W),
-        enter_row=room(2, 2, 3, W),
         halo=room(2, 3, K, W),
         edge_out=half(G, 2, 3, K, W),
         edge_in=half(G, 2, 3, K, W),

time: 27.9 us -> 27.6 us (0.989)
  Pallas kernels: 27 us -> 26.7 us
    pallas_call x1, Pallas kernels: 27 us -> 26.7 us  [per_device(): pl.pallas_call(functools.partial(kernel, S, N, tuple(scratch)), out_shape...]
where the time goes in v7:
time: 27.6 us; the launch traced here: 27.4 us
  Pallas kernels  26.7 us (97%)
  local copies, waits for them, and re-layouts  0.75 us (3%)
    pallas_call x1, Pallas kernels, per_device(): pl.pallas_call(functools.partial(kernel, S, N, tuple(scratch)), out_shape...  26.7 us
    unnamed x1, local copies, waits for them, and re-layouts  0.75 us

profile of v7, /device:TPU:0, one launch (start us, length us, event | category | flops | bytes accessed | tf_op | source)
XLA Modules:
  0.0 27.4 jit_solution(12563294767224590016)
XLA Ops:
  0.0 26.7 %line_sweeps.1 = f32[16,3,8,256]{3,2,1,0:T(8,128)S(1)} custom-call(f32[128]{0:T(128)} %amplitude_hbm.1, s32[128]{0:T(128)} %mode_patch_hbm.1, s32[64,256]{1,0:T(8,128)} %column_patch_hbm.1, s32[8,256]{1,0:T(8,128)} %wall_mask_hbm.1, s32[8,256]{1,0:T(8,128)} %offsets_hbm.1, bf16[16,3,64,256]{3,2,1,0:T(8,128)(2,1)} %bitcast.4, f32[16,8,256]{2,1,0:T(8,128)} %coupling_hbm.1, ...), custom_call_target="tpu_custom_call" | custom-call | tf_op jit(solution)/shard_map/line_sweeps/pallas_call | solution.py:746
  26.7 0.7 %copy.11 = f32[16,8,3,256]{3,1,2,0:T(8,128)} copy(f32[16,8,3,256]{3,1,2,0:T(8,128)S(1)} %bitcast.3) | data formatting | bytes 786432

commit v8 on v7

--- a/solution.py
+++ b/solution.py
@@ -584,7 +584,7 @@
             put(out, k, state)
             return carry
 
-        loop(K, finish, 0, 8)
+        loop(K, finish, 0, K)
 
         if sweep == 0:
 

time: 27.6 us -> 27.6 us (level)
  no operation moved by 1% of the time
where the time goes in v8:
time: 27.6 us; the launch traced here: 27.4 us
  Pallas kernels  26.7 us (97%)
  local copies, waits for them, and re-layouts  0.75 us (3%)
    pallas_call x1, Pallas kernels, per_device(): pl.pallas_call(functools.partial(kernel, S, N, tuple(scratch)), out_shape...  26.7 us
    unnamed x1, local copies, waits for them, and re-layouts  0.75 us

profile of v8, /device:TPU:0, one launch (start us, length us, event | category | flops | bytes accessed | tf_op | source)
XLA Modules:
  0.0 27.4 jit_solution(12539474770577178361)
XLA Ops:
  0.0 26.7 %line_sweeps.1 = f32[16,3,8,256]{3,2,1,0:T(8,128)S(1)} custom-call(f32[128]{0:T(128)} %amplitude_hbm.1, s32[128]{0:T(128)} %mode_patch_hbm.1, s32[64,256]{1,0:T(8,128)} %column_patch_hbm.1, s32[8,256]{1,0:T(8,128)} %wall_mask_hbm.1, s32[8,256]{1,0:T(8,128)} %offsets_hbm.1, bf16[16,3,64,256]{3,2,1,0:T(8,128)(2,1)} %bitcast.4, f32[16,8,256]{2,1,0:T(8,128)} %coupling_hbm.1, ...), custom_call_target="tpu_custom_call" | custom-call | tf_op jit(solution)/shard_map/line_sweeps/pallas_call | solution.py:746
  26.7 0.7 %copy.11 = f32[16,8,3,256]{3,1,2,0:T(8,128)} copy(f32[16,8,3,256]{3,1,2,0:T(8,128)S(1)} %bitcast.3) | data formatting | bytes 786432
